TPU v7x, 32 devices: a whole 2x2x4 slice. The times are simulated.
32 devices in a mesh: shot: 8 (over y, x, core), tm: 4 (over z).
Axes of the slice: x: 2, y: 2, z: 4, core: 2. Of those that a mesh axis runs over, the one named last changes fastest.
Arguments:
- records: bfloat16 [8, 16, 512], P('shot', None, 'tm'), may hold values from -6 to 6
- live: int32 [8, 16], P('shot'), may hold values 0 or 1
- dither: int32 [8], replicated, may hold values from 0 to 32, as said below
- designature: bfloat16 [9, 33], replicated, may hold values from -0.375 to 0.375
- first_weights: bfloat16 [64, 30], replicated, may hold values from -1.5 to 1.5
- first_bias: float32 [64], replicated, may hold values from -2.5 to 2.5
- hidden_weights: bfloat16 [3, 64, 192], replicated, may hold values from -0.625 to 0.625
- hidden_bias: float32 [3, 64], replicated, may hold values from -2.5 to 2.5
- out_weights: bfloat16 [64], replicated, may hold values from -0.75 to 0.75
- out_bias: float32 [1], replicated, may hold values from -2.5 to 2.5
- shaping: bfloat16 [9, 33], replicated, may hold values from -0.375 to 0.375
Outputs:
- interference: bfloat16 [8, 16, 512], P('shot', None, 'tm')
- cleaned: bfloat16 [8, 16, 512], P('shot', None, 'tm')
Inputs may be any that keep to these rules, and one draw needn't show every extreme that they name: One shot's dither is exactly 32 and one shot's is 0.
All inputs are finite; a program needn't handle non-finite values. No bound on the sum of `live` on one device may be relied on, other than what follows from the above.
Results may differ from a plain program's by a relative error of at most 0.012.
The roundings to bfloat16 on the way count: a program that leaves them out, or rounds other values in their place, can miss the bound.
Values may be sent and summed in bfloat16 or wider, within the bound.
No kernel may reach another device: no remote copies, remote signals or barrier semaphores. Data moves between devices by JAX's collectives and lax.ppermute only.
A program may use at most 64 MiB of HBM per device.

v0:
```python
import jax
import jax.numpy as jnp
from jax import lax
from jax.sharding import PartitionSpec as P

HID = 3
FN = 9
FT = 33
SHOT_TAPS = 5
DMAX = 32


def extended_2(array, sides, width):
    for axis, dim in sides:
        devices, length = (lax.axis_size(axis), array.shape[dim])
        up = [(i, (i + 1) % devices) for i in range(devices - 1)]
        down = [(j, i) for i, j in up]
        last = lax.slice_in_dim(array, length - width, length, axis=dim)
        leading = lax.slice_in_dim(array, 0, width, axis=dim)
        before = lax.ppermute(last, axis, up)
        after = lax.ppermute(leading, axis, down)
        array = jnp.concatenate([before, array, after], axis=dim)
    return array


def apply_taps(rimmed, taps):
    shots_here, nodes, length = rimmed.shape
    samples = length - (FT - 1)
    node_pad = jnp.pad(rimmed, ((0, 0), (FN // 2, FN // 2), (0, 0)))
    shifted = jnp.stack([node_pad[:, offset : offset + nodes, :] for offset in range(FN)], axis=2)
    partial_rows = jnp.einsum("snal,ab->snbl", shifted, taps, preferred_element_type=jnp.float32)
    total_sum = partial_rows[:, :, 0, 0:samples]
    for shift in range(1, FT):
        total_sum = total_sum + partial_rows[:, :, shift, shift : shift + samples]
    return total_sum


def valid_mask(width, samples, first_sample, total):
    margin = (width - samples) // 2
    positions = first_sample + jnp.arange(width, dtype=jnp.int32) - margin
    return (positions >= 0) & (positions < total)


def predict(
    gather_rows,
    dither_rows,
    first_weights,
    first_bias,
    hidden_weights,
    hidden_bias,
    out_weights,
    out_bias,
    samples,
    first_sample,
    total,
):
    rows_in = gather_rows.shape[1]
    rows_out = rows_in - 2 * (SHOT_TAPS // 2)
    reach_full = 2 ** (HID + 1) - 1
    extended = extended_2(gather_rows, (("tm", 2),), DMAX + reach_full)
    span = samples + 2 * reach_full
    direct = extended[:, :, DMAX : DMAX + span]
    shift_rows = jax.vmap(lambda row, delay: lax.dynamic_slice_in_dim(row, DMAX + delay, span))
    retimed = jax.vmap(shift_rows, in_axes=(0, None))(extended, dither_rows)
    inputs = jnp.stack([direct, retimed])
    inputs = jnp.where(
        valid_mask(span, samples, first_sample, total)[None, None, None, :],
        inputs,
        jnp.zeros_like(inputs),
    )
    width = span - 2
    columns = jnp.stack(
        [
            inputs[channel, :, offset : offset + rows_out, shift : shift + width]
            for channel in range(2)
            for offset in range(SHOT_TAPS)
            for shift in range(3)
        ]
    )
    summed = jnp.einsum("of,fgst->ogst", first_weights, columns, preferred_element_type=jnp.float32)
    summed = summed + first_bias[:, None, None, None]
    keep_time = valid_mask(width, samples, first_sample, total)[None, None, None, :]
    active = jnp.where(keep_time, jax.nn.relu(summed), 0.0).astype(jnp.bfloat16)
    for layer in range(HID):
        dilation = 2 ** (layer + 1)
        width = active.shape[3] - 2 * dilation
        stacked = jnp.concatenate(
            [active[:, :, :, shift * dilation : shift * dilation + width] for shift in range(3)],
            axis=0,
        )
        summed = jnp.einsum(
            "of,fgst->ogst", hidden_weights[layer], stacked, preferred_element_type=jnp.float32
        )
        summed = summed + hidden_bias[layer][:, None, None, None]
        keep_time = valid_mask(width, samples, first_sample, total)[None, None, None, :]
        active = jnp.where(keep_time, jax.nn.relu(summed), 0.0).astype(jnp.bfloat16)
    result = (
        jnp.einsum("c,cgst->gst", out_weights, active, preferred_element_type=jnp.float32)
        + out_bias[0]
    )
    return result.astype(jnp.bfloat16)


def local(
    records,
    live,
    dither,
    designature,
    first_weights,
    first_bias,
    hidden_weights,
    hidden_bias,
    out_weights,
    out_bias,
    shaping,
):
    samples = records.shape[2]
    total = samples * lax.axis_size("tm")
    first_sample = lax.axis_index("tm") * samples
    margin_rows = SHOT_TAPS // 2
    keep = live[:, :, None] > 0
    masked = jnp.where(keep, records, jnp.zeros_like(records))
    rimmed = extended_2(masked, (("tm", 2),), FT // 2)
    filtered = jnp.where(keep, apply_taps(rimmed, designature), 0.0).astype(jnp.bfloat16)
    padded_dither = jnp.pad(dither, ((margin_rows, margin_rows),))
    weights = (first_weights, first_bias, hidden_weights, hidden_bias, out_weights, out_bias)
    gathers = lax.all_to_all(filtered, "shot", split_axis=1, concat_axis=0, tiled=True)
    by_node = jnp.pad(
        jnp.transpose(gathers, (1, 0, 2)), ((0, 0), (margin_rows, margin_rows), (0, 0))
    )
    predicted = predict(by_node, padded_dither, *weights, samples, first_sample, total)
    predicted = jnp.transpose(predicted, (1, 0, 2))
    returned = lax.all_to_all(predicted, "shot", split_axis=0, concat_axis=1, tiled=True)
    interference = jnp.where(keep, returned, jnp.zeros_like(returned))
    deblended = (filtered.astype(jnp.float32) - interference.astype(jnp.float32)).astype(
        jnp.bfloat16
    )
    rimmed_again = extended_2(deblended, (("tm", 2),), FT // 2)
    cleaned = jnp.where(keep, apply_taps(rimmed_again, shaping), 0.0).astype(jnp.bfloat16)
    return (interference, cleaned)


def solution(mesh):
    in_specs = (P("shot", None, "tm"), P("shot", None), P(), P(), P(), P(), P(), P(), P(), P(), P())
    out_specs = (P("shot", None, "tm"), P("shot", None, "tm"))
    return jax.shard_map(local, mesh=mesh, in_specs=in_specs, out_specs=out_specs, check_vma=False)
```

profile of v0, /device:TPU:0, one launch (start us, length us, event | category | flops | bytes accessed | tf_op | source)
XLA Modules:
  0.0 60.7 jit_solution(3704261095584289838)
XLA Ops:
  0.6 0.7 %compare_bitcast_fusion = pred[16]{0:T(512)(128)(4,1)S(1)} fusion(s32[1,16]{1,0:T(1,128)} %param.12), kind=kLoop, calls=%fused_computation.183 | loop fusion | flops 16 | bytes 80 | tf_op jit(solution)/shard_map/gt | solution.py:121
  1.3 0.8 %broadcast_select_fusion.1 = bf16[1,16,128]{2,1,0:T(8,128)(2,1)S(1)} fusion(bf16[1,16,128]{2,1,0:T(8,128)(2,1)} %param.11, pred[16]{0:T(512)(128)(4,1)S(1)} %compare_bitcast_fusion), kind=kLoop, calls=%fused_computation.176 | loop fusion | flops 2048 | bytes 8208 | tf_op jit(solution)/shard_map/jit(_where)/select_n | solution.py:122
  2.1 4.9 %collective-permute-start = (bf16[1,16,16]{2,1,0:T(8,128)(2,1)S(1)}, bf16[1,16,16]{2,1,0:T(8,128)(2,1)S(1)}, u32[]{:S(2)}, u32[]{:S(2)}) collective-permute-start(bf16[1,16,16]{2,1,0:T(8,128)(2,1)S(1)} %get-tuple-element.88), channel_id=1, source_target_pairs={{0,1},{1,2},{2,3},{4,5},{5,6},{6,7},{8,9},{9,10},{10,11},{12,13},{... | collective-permute-start | bytes 1544 | tf_op jit(solution)/shard_map/ppermute | solution.py:20
  7.1 1.3 %collective-permute-start.1 = (bf16[1,16,16]{2,1,0:T(8,128)(2,1)S(1)}, bf16[1,16,16]{2,1,0:T(8,128)(2,1)S(1)}, u32[]{:S(2)}, u32[]{:S(2)}) collective-permute-start(bf16[1,16,16]{2,1,0:T(8,128)(2,1)S(1)} %get-tuple-element.89), channel_id=1, source_target_pairs={{1,0},{2,1},{3,2},{5,4},{6,5},{7,6},{9,8},{10,9},{11,10},{13,12},{... | collective-permute-start | bytes 1544 | tf_op jit(solution)/shard_map/ppermute | solution.py:21
  8.4 0.8 %slice_bitcast_fusion.17 = (f32[64]{0:T(128)S(1)}, f32[64]{0:T(128)S(1)}, f32[64]{0:T(128)S(1)}) fusion(f32[3,64]{1,0:T(4,128)} %param.18), kind=kLoop, calls=%fused_computation.188 | loop fusion | bytes 1536 | tf_op jit(solution)/shard_map/add | solution.py:94
  9.3 3.3 %collective-permute-done.1 = bf16[1,16,16]{2,1,0:T(8,128)(2,1)S(1)} collective-permute-done((bf16[1,16,16]{2,1,0:T(8,128)(2,1)S(1)}, bf16[1,16,16]{2,1,0:T(8,128)(2,1)S(1)}, u32[]{:S(2)}, u32[]{:S(2)}) %collective-permute-start.1) | collective-permute-done | bytes 544 | tf_op jit(solution)/shard_map/ppermute | solution.py:21
  13.2 1.0 %convolution_bitcast_fusion = f32[1,16,33,160]{3,2,1,0:T(8,128)S(1)} fusion(bf16[1,16,9,160]{3,2,1,0:T(8,128)(2,1)S(1)} %stack.81, bf16[9,33]{1,0:T(8,128)(2,1)} %param.14), kind=kOutput, calls=%fused_computation.25 | convolution fusion | flops 1520640 | bytes 384594 | tf_op jit(solution)/shard_map/snal,ab->snbl/dot_general | solution.py:31
  15.0 0.6 copy.375
  15.6 3.7 %all-to-all-start = ((bf16[8,2,128]{2,1,0:T(2,128)(2,1)}), bf16[8,2,128]{2,1,0:T(2,128)(2,1)S(1)}, u32[]{:S(2)}, u32[]{:S(2)}) async-start(bf16[8,2,128]{2,1,0:T(2,128)(2,1)} %bitcast.357), calls=%async_computation | async-start | bytes 8192 | tf_op jit(solution)/shard_map/all_to_all | solution.py:127
  19.3 4.6 %all-to-all-done = bf16[8,2,128]{2,1,0:T(2,128)(2,1)S(1)} async-done(((bf16[8,2,128]{2,1,0:T(2,128)(2,1)}), bf16[8,2,128]{2,1,0:T(2,128)(2,1)S(1)}, u32[]{:S(2)}, u32[]{:S(2)}) %all-to-all-start) | async-done | bytes 4128 | tf_op jit(solution)/shard_map/all_to_all | solution.py:127
  24.0 3.5 %collective-permute-start.2 = (bf16[2,12,47]{2,0,1:T(2,128)(2,1)S(1)}, bf16[2,12,47]{2,0,1:T(2,128)(2,1)S(1)}, u32[]{:S(2)}, u32[]{:S(2)}) collective-permute-start(bf16[2,12,47]{2,0,1:T(2,128)(2,1)S(1)} %get-tuple-element.86), channel_id=1, source_target_pairs={{0,1},{1,2},{2,3},{4,5},{5,6},{6,7},{8,9},{9,10},{10,11},{12,13},{... | collective-permute-start | bytes 6776 | tf_op jit(solution)/shard_map/ppermute | solution.py:20
  27.5 1.3 %collective-permute-start.3 = (bf16[2,12,47]{2,0,1:T(2,128)(2,1)S(1)}, bf16[2,12,47]{2,0,1:T(2,128)(2,1)S(1)}, u32[]{:S(2)}, u32[]{:S(2)}) collective-permute-start(bf16[2,12,47]{2,0,1:T(2,128)(2,1)S(1)} %get-tuple-element.87), channel_id=1, source_target_pairs={{1,0},{2,1},{3,2},{5,4},{6,5},{7,6},{9,8},{10,9},{11,10},{13,12},{... | collective-permute-start | bytes 6776 | tf_op jit(solution)/shard_map/ppermute | solution.py:21
  29.6 3.5 %collective-permute-done.3 = bf16[2,12,47]{2,0,1:T(2,128)(2,1)S(1)} collective-permute-done((bf16[2,12,47]{2,0,1:T(2,128)(2,1)S(1)}, bf16[2,12,47]{2,0,1:T(2,128)(2,1)S(1)}, u32[]{:S(2)}, u32[]{:S(2)}) %collective-permute-start.3) | collective-permute-done | bytes 2288 | tf_op jit(solution)/shard_map/ppermute | solution.py:21
  33.1 0.9 %copy.315 = bf16[2,12,222]{0,1,2:T(8,128)(2,1)S(1)} copy(bf16[2,12,222]{2,0,1:T(2,128)(2,1)S(1)} %pad_maximum_fusion) | data formatting | bytes 21312 | tf_op jit(solution)/shard_map/concatenate | solution.py:22
  34.1 2.5 %gather_fusion = bf16[12,2,158]{1,0,2:T(8,128)(2,1)S(1)} fusion(bf16[2,12,222]{0,1,2:T(8,128)(2,1)S(1)} %copy.315, s32[12]{0:T(128)S(1)} %fusion.134), kind=kCustom, calls=%fused_computation | custom fusion | bytes 15264 | tf_op jit(solution)/shard_map/vmap(vmap())/gather | solution.py:63
  36.7 0.7 %copy.318 = bf16[1,2,12,158]{3,0,2,1:T(2,128)(2,1)S(1)} copy(bf16[1,2,12,158]{1,2,3,0:T(8,128)(2,1)S(1)} %bitcast.360) | data formatting | bytes 15168 | tf_op jit(solution)/shard_map/stack | solution.py:65
  38.0 0.9 %stack.85 = bf16[30,2,8,156]{3,0,2,1:T(8,128)(2,1)S(1)} concatenate(bf16[1,2,8,156]{3,0,2,1:T(2,128)(2,1)S(1)} %get-tuple-element.75, bf16[1,2,8,156]{3,0,2,1:T(2,128)(2,1)S(1)} %get-tuple-element.74, bf16[1,2,8,156]{3,0,2,1:T(2,128)(2,1)S(1)} %get-tuple-element.73, bf16[1,2,8,156]{3,0,2,1:T(2,128)(2,1)S(1)} %get-tuple-element.72, bf16[1,2,8,156]{3,0,2,1:T(2,128)(2,1)S(1)} %get-tuple-element.71, ...), dimensions={0} | concatenate | bytes 299520 | tf_op jit(solution)/shard_map/stack | solution.py:72
  39.7 0.5 copy-done.2
  42.5 7.0 %all_to_all.24 = bf16[8,2,128]{2,1,0:T(2,128)(2,1)S(1)} all-to-all(bf16[8,2,128]{2,1,0:T(2,128)(2,1)S(1)} %fusion.129), channel_id=1, replica_groups=mesh['shot'=8,'tm'=4] {'shot'}, dimensions={0} | all-to-all | bytes 8192 | tf_op jit(solution)/shard_map/all_to_all | solution.py:133
  49.6 0.7 %subtract_convert_fusion = (bf16[1,16,128]{2,1,0:T(8,128)(2,1)S(1)}, bf16[1,16,128]{2,1,0:T(8,128)(2,1)}) fusion(bf16[1,16,128]{2,1,0:T(8,128)(2,1)S(1)} %fusion.128, pred[16]{0:T(512)(128)(4,1)S(1)} %compare_bitcast_fusion, bf16[1,16,128]{2,1,0:T(8,128)(2,1)S(1)} %bitcast.399), kind=kLoop, calls=%fused_computation.170 | loop fusion | flops 10240 | bytes 16400 | tf_op jit(solution)/shard_map/convert_element_type | solution.py:135
  50.3 3.5 %collective-permute-start.4 = (bf16[1,16,16]{2,1,0:T(8,128)(2,1)S(1)}, bf16[1,16,16]{2,1,0:T(8,128)(2,1)S(1)}, u32[]{:S(2)}, u32[]{:S(2)}) collective-permute-start(bf16[1,16,16]{2,1,0:T(8,128)(2,1)S(1)} %get-tuple-element.84), channel_id=1, source_target_pairs={{0,1},{1,2},{2,3},{4,5},{5,6},{6,7},{8,9},{9,10},{10,11},{12,13},{... | collective-permute-start | bytes 1544 | tf_op jit(solution)/shard_map/ppermute | solution.py:20
  53.8 1.3 %collective-permute-start.5 = (bf16[1,16,16]{2,1,0:T(8,128)(2,1)S(1)}, bf16[1,16,16]{2,1,0:T(8,128)(2,1)S(1)}, u32[]{:S(2)}, u32[]{:S(2)}) collective-permute-start(bf16[1,16,16]{2,1,0:T(8,128)(2,1)S(1)} %get-tuple-element.85), channel_id=1, source_target_pairs={{1,0},{2,1},{3,2},{5,4},{6,5},{7,6},{9,8},{10,9},{11,10},{13,12},{... | collective-permute-start | bytes 1544 | tf_op jit(solution)/shard_map/ppermute | solution.py:21
  55.1 4.2 %collective-permute-done.5 = bf16[1,16,16]{2,1,0:T(8,128)(2,1)S(1)} collective-permute-done((bf16[1,16,16]{2,1,0:T(8,128)(2,1)S(1)}, bf16[1,16,16]{2,1,0:T(8,128)(2,1)S(1)}, u32[]{:S(2)}, u32[]{:S(2)}) %collective-permute-start.5) | collective-permute-done | bytes 544 | tf_op jit(solution)/shard_map/ppermute | solution.py:21
  60.0 0.7 %fusion.93 = bf16[1,16,128]{2,1,0:T(8,128)(2,1)} fusion(f32[1,16,33,160]{3,1,2,0:T(8,128)S(1)} %bitcast.359, pred[16]{0:T(512)(128)(4,1)S(1)} %compare_bitcast_fusion), kind=kLoop, calls=%fused_computation.100 | loop fusion | flops 69632 | bytes 274448 | tf_op jit(solution)/shard_map/convert_element_type | solution.py:139
  (69 shorter events, 6.2 us)
Async XLA Ops:
  0.6 38.3 %copy-start = (bf16[64,30]{0,1:T(8,128)(2,1)S(1)}, bf16[64,30]{0,1:T(8,128)(2,1)}, u32[]{:S(2)}) copy-start(bf16[64,30]{0,1:T(8,128)(2,1)} %param.15) | copy-start | bytes 11524
  2.1 7.1 %collective-permute-start = (bf16[1,16,16]{2,1,0:T(8,128)(2,1)S(1)}, bf16[1,16,16]{2,1,0:T(8,128)(2,1)S(1)}, u32[]{:S(2)}, u32[]{:S(2)}) collective-permute-start(bf16[1,16,16]{2,1,0:T(8,128)(2,1)S(1)} %get-tuple-element.88), channel_id=1, source_target_pairs={{0,1},{1,2},{2,3},{4,5},{5,6},{6,7},{8,9},{9,10},{10,11},{12,13},{... | collective-permute-start | bytes 1544 | tf_op jit(solution)/shard_map/ppermute | solution.py:20
  7.1 5.5 %collective-permute-start.1 = (bf16[1,16,16]{2,1,0:T(8,128)(2,1)S(1)}, bf16[1,16,16]{2,1,0:T(8,128)(2,1)S(1)}, u32[]{:S(2)}, u32[]{:S(2)}) collective-permute-start(bf16[1,16,16]{2,1,0:T(8,128)(2,1)S(1)} %get-tuple-element.89), channel_id=1, source_target_pairs={{1,0},{2,1},{3,2},{5,4},{6,5},{7,6},{9,8},{10,9},{11,10},{13,12},{... | collective-permute-start | bytes 1544 | tf_op jit(solution)/shard_map/ppermute | solution.py:21
  13.2 15.6 %copy-start.3 = (s32[8]{0:T(128)S(1)}, s32[8]{0:T(128)}, u32[]{:S(2)}) copy-start(s32[8]{0:T(128)} %param.13) | copy-start | bytes 100
  15.6 8.3 %all-to-all-start = ((bf16[8,2,128]{2,1,0:T(2,128)(2,1)}), bf16[8,2,128]{2,1,0:T(2,128)(2,1)S(1)}, u32[]{:S(2)}, u32[]{:S(2)}) async-start(bf16[8,2,128]{2,1,0:T(2,128)(2,1)} %bitcast.357), calls=%async_computation | async-start | bytes 8192 | tf_op jit(solution)/shard_map/all_to_all | solution.py:127
  24.0 5.5 %collective-permute-start.2 = (bf16[2,12,47]{2,0,1:T(2,128)(2,1)S(1)}, bf16[2,12,47]{2,0,1:T(2,128)(2,1)S(1)}, u32[]{:S(2)}, u32[]{:S(2)}) collective-permute-start(bf16[2,12,47]{2,0,1:T(2,128)(2,1)S(1)} %get-tuple-element.86), channel_id=1, source_target_pairs={{0,1},{1,2},{2,3},{4,5},{5,6},{6,7},{8,9},{9,10},{10,11},{12,13},{... | collective-permute-start | bytes 6776 | tf_op jit(solution)/shard_map/ppermute | solution.py:20
  27.5 5.5 %collective-permute-start.3 = (bf16[2,12,47]{2,0,1:T(2,128)(2,1)S(1)}, bf16[2,12,47]{2,0,1:T(2,128)(2,1)S(1)}, u32[]{:S(2)}, u32[]{:S(2)}) collective-permute-start(bf16[2,12,47]{2,0,1:T(2,128)(2,1)S(1)} %get-tuple-element.87), channel_id=1, source_target_pairs={{1,0},{2,1},{3,2},{5,4},{6,5},{7,6},{9,8},{10,9},{11,10},{13,12},{... | collective-permute-start | bytes 6776 | tf_op jit(solution)/shard_map/ppermute | solution.py:21
  37.5 1.4 %copy-start.4 = (f32[64]{0:T(128)S(1)}, f32[64]{0:T(128)}, u32[]{:S(2)}) copy-start(f32[64]{0:T(128)} %param.16) | copy-start | bytes 772
  39.3 0.9 %copy-start.2 = (bf16[3,64,192]{2,1,0:T(8,128)(2,1)S(1)}, bf16[3,64,192]{2,1,0:T(8,128)(2,1)}, u32[]{:S(2)}) copy-start(bf16[3,64,192]{2,1,0:T(8,128)(2,1)} %param.17) | copy-start | bytes 221188
  41.5 0.7 %copy-start.5 = (bf16[64]{0:T(256)(128)(2,1)S(1)}, bf16[64]{0:T(256)(128)(2,1)}, u32[]{:S(2)}) copy-start(bf16[64]{0:T(256)(128)(2,1)} %param.19) | copy-start | bytes 388
  42.1 17.4 %copy-start.1 = (bf16[9,33]{1,0:T(8,128)(2,1)S(1)}, bf16[9,33]{1,0:T(8,128)(2,1)}, u32[]{:S(2)}) copy-start(bf16[9,33]{1,0:T(8,128)(2,1)} %param.21) | copy-start | bytes 1786
  50.3 4.8 %collective-permute-start.4 = (bf16[1,16,16]{2,1,0:T(8,128)(2,1)S(1)}, bf16[1,16,16]{2,1,0:T(8,128)(2,1)S(1)}, u32[]{:S(2)}, u32[]{:S(2)}) collective-permute-start(bf16[1,16,16]{2,1,0:T(8,128)(2,1)S(1)} %get-tuple-element.84), channel_id=1, source_target_pairs={{0,1},{1,2},{2,3},{4,5},{5,6},{6,7},{8,9},{9,10},{10,11},{12,13},{... | collective-permute-start | bytes 1544 | tf_op jit(solution)/shard_map/ppermute | solution.py:20
  53.8 5.5 %collective-permute-start.5 = (bf16[1,16,16]{2,1,0:T(8,128)(2,1)S(1)}, bf16[1,16,16]{2,1,0:T(8,128)(2,1)S(1)}, u32[]{:S(2)}, u32[]{:S(2)}) collective-permute-start(bf16[1,16,16]{2,1,0:T(8,128)(2,1)S(1)} %get-tuple-element.85), channel_id=1, source_target_pairs={{1,0},{2,1},{3,2},{5,4},{6,5},{7,6},{9,8},{10,9},{11,10},{13,12},{... | collective-permute-start | bytes 1544 | tf_op jit(solution)/shard_map/ppermute | solution.py:21
where the time goes:
time: 61.2 us; the launch traced here: 60.7 us
  starting transfers between devices  19.5 us (32%)
  waiting for transfers between devices  15.6 us (25%)
  local copies, waits for them, and re-layouts  10.5 us (17%)
  blocking collectives  7.04 us (12%)
  other arithmetic  3.45 us (6%)
  matrix products  2.85 us (5%)
  between operations  1.72 us (3%)
    ppermute x3, starting transfers between devices, extended_2(): before = lax.ppermute(last, axis, up)  11.9 us
    ppermute x3, waiting for transfers between devices, extended_2(): after = lax.ppermute(leading, axis, down)  11 us
    all_to_all x1, blocking collectives, local(): lax.all_to_all(predicted, 'shot', split_axis=0, concat_axis=1, tiled=True)  7.04 us
    all_to_all x1, waiting for transfers between devices, local(): lax.all_to_all(filtered, 'shot', split_axis=1, concat_axis=0, tiled=True)  4.6 us
    ppermute x3, starting transfers between devices, extended_2(): after = lax.ppermute(leading, axis, down)  3.88 us
    all_to_all x1, starting transfers between devices, local(): lax.all_to_all(filtered, 'shot', split_axis=1, concat_axis=0, tiled=True)  3.73 us
    gather x1, local copies, waits for them, and re-layouts, predict(): lax.dynamic_slice_in_dim(row, DMAX + delay, span)  2.51 us
    unnamed x23, local copies, waits for them, and re-layouts  1.6 us
  transfers between devices with their start and end apart: 7, of which 4 were waited for; matrix products, arithmetic and copies ran while one was open for 2% of the time, Pallas kernels for 0%

commit v1 on v0

v1 whole, which is shorter than its diff:
```python
import functools

import jax
import jax.numpy as jnp
from jax import lax
from jax.experimental import pallas as pl
from jax.experimental.pallas import tpu as pltpu
from jax.sharding import PartitionSpec as P

HID = 3
FN = 9
FT = 33
SHOT_TAPS = 5
DMAX = 32
LANES = 128
LEAD = 32
DEAD = 3e38
LIMIT = 1e38
F32 = jnp.float32
BF16 = jnp.bfloat16
AXES = ("shot", "tm")


def partners(shots, parts, rule):
    out = []
    for s in range(shots):
        for t in range(parts):
            a, b = rule(s, t)
            out.append((s * parts + t, a * parts + b))
    return out


def exchanges(shots, parts):
    def time_odd(s, t):
        o = ((t + 1) ^ 1) - 1
        return (s, o) if 0 <= o < parts else (s ^ 1, t)

    def pair_odd(s, t):
        o = ((s // 2 + 1) ^ 1) - 1
        return (2 * o + s % 2, t) if 0 <= o < shots // 2 else (s ^ 1, t)

    rules = (
        lambda s, t: (s, t ^ 1),
        time_odd,
        lambda s, t: (s ^ 1, t),
        lambda s, t: (s ^ 2, t),
        pair_odd,
    )
    return [partners(shots, parts, rule) for rule in rules]


def contract_lanes(a, b):
    return lax.dot_general(a, b, (((1,), (1,)), ((), ())), preferred_element_type=F32)


def prepare(info, designature, shaping, first_weights, biases, out_weights, tt1, tt2, w0, ow, bt, pad):
    window = tt1.shape[1]
    for taps, offset, out in ((designature, window - LANES - LEAD - FT // 2, tt1), (shaping, LEAD - FT // 2, tt2)):
        pad[...] = jnp.zeros_like(pad)
        pad[0:FN, 0:FT] = taps[...].astype(F32)
        for a in range(FN):
            row = jnp.broadcast_to(pad[a : a + 1, :], (LANES, window))
            row = pltpu.roll(row, offset, 1, stride=1, stride_axis=0)
            out[a * LANES : (a + 1) * LANES, :] = row.astype(BF16)
    parity = info[1] % 2
    columns = first_weights.shape[1]
    f = lax.broadcasted_iota(jnp.int32, (columns, w0.shape[1]), 0)
    g = lax.broadcasted_iota(jnp.int32, (columns, w0.shape[1]), 1)
    c, a, k = f // (3 * SHOT_TAPS), (f // 3) % SHOT_TAPS, f % 3
    here = (g // 16 == k) & ((g // 8) % 2 == c) & (g % 8 == a + parity)
    select = jnp.where(here, 1.0, 0.0).astype(BF16)
    w0[...] = jnp.dot(first_weights[...], select, preferred_element_type=F32).astype(BF16)
    channels = out_weights.shape[1]
    nodes = ow.shape[0]
    row = out_weights[...].astype(F32)
    row = jnp.concatenate([row] * (LANES // channels), axis=1)
    n = lax.broadcasted_iota(jnp.int32, (nodes, LANES), 0)
    for i in range(ow.shape[1] // LANES):
        m = (lax.broadcasted_iota(jnp.int32, (nodes, LANES), 1) + i * LANES) // channels
        ow[:, i * LANES : (i + 1) * LANES] = jnp.where(m == n, jnp.broadcast_to(row, n.shape), 0.0).astype(BF16)
    pad[...] = jnp.zeros_like(pad)
    pad[0 : biases.shape[0], 0:channels] = biases[...]
    bt[...] = jnp.transpose(pad[0:8, 0:LANES])


def deblend(
    total,
    shots,
    info,
    dither,
    out_bias,
    pair,
    first,
    second,
    tt1,
    tt2,
    w0,
    hidden,
    bt,
    ow,
    interference,
    cleaned,
    xs,
    yp,
    gs,
    zp,
):
    nodes, samples = interference.shape
    windows = samples // LANES + 1
    span = windows * LANES
    window = 2 * LANES
    channels = w0.shape[0]
    t, s = info[0], info[1]
    chip = s // 2
    even = chip % 2 == 0
    lowest, highest = chip == 0, chip == shots // 2 - 1
    stride = nodes + 8
    live = []
    for j in range(6):
        if 2 <= j < 4:
            x = pair[j - 2].astype(F32)
        else:
            p, q = (second, first) if j < 2 else (first, second)
            x = jnp.where(even, p[j % 2].astype(F32), q[j % 2].astype(F32))
            x = jnp.where(lowest if j < 2 else highest, 0.0, x)
        live.append(x[:, LANES : LANES + 1] < LIMIT)
        x = jnp.where(x < LIMIT, x, 0.0).astype(BF16)
        for w in range(windows):
            row = (w * 6 + j) * nodes
            xs[row : row + nodes, :] = x[:, w * LANES : w * LANES + window]
    blocks = windows * 6
    yp[...] = jnp.zeros_like(yp)
    y = contract_lanes(xs[...], tt1[...])
    for q in range(blocks):
        yp[8 + q * stride : 8 + q * stride + nodes, :] = y[q * nodes : (q + 1) * nodes, :]
    position = t * samples - LEAD + lax.broadcasted_iota(jnp.int32, (1, span), 1)
    valid = (position >= 0) & (position < total)
    gs[...] = jnp.zeros_like(gs)
    filtered = []
    for j in range(6):
        tiles = []
        for w in range(windows):
            base = 8 + (w * 6 + j) * stride - FN // 2
            acc = None
            for a in range(FN):
                v = yp[base + a : base + a + nodes, a * LANES : (a + 1) * LANES]
                acc = v if acc is None else acc + v
            tiles.append(acc)
        f = jnp.concatenate(tiles, axis=1)
        f = jnp.where(live[j] & valid, f, 0.0).astype(BF16).astype(F32)
        filtered.append(f)
        shot = jnp.clip(2 * chip - 2 + j, 0, shots - 1)
        r = pltpu.roll(f, span - dither[shot], 1)
        r = jnp.where(valid, r, 0.0)
        for w in range(windows):
            row = w * nodes * 16 + j
            gs[pl.ds(row, nodes, stride=16), :] = f[:, w * LANES : (w + 1) * LANES]
            gs[pl.ds(row + 8, nodes, stride=16), :] = r[:, w * LANES : (w + 1) * LANES]
    g = jnp.concatenate([gs[w * nodes * 16 : (w + 1) * nodes * 16, :] for w in range(windows)], axis=1)
    shifted = [pltpu.roll(g, 1, 1).astype(BF16), g.astype(BF16), pltpu.roll(g, span - 1, 1).astype(BF16)]
    acts = []
    for n in range(nodes):
        columns = jnp.concatenate([v[16 * n : 16 * n + 16, :] for v in shifted], axis=0)
        act = jnp.dot(w0[...], columns, preferred_element_type=F32) + bt[0:channels, 0:1]
        act = jnp.where(valid, jnp.maximum(act, 0.0), 0.0)
        for layer in range(HID):
            e = 2 ** (layer + 1)
            columns = jnp.concatenate(
                [pltpu.roll(act, e, 1).astype(BF16), act.astype(BF16), pltpu.roll(act, span - e, 1).astype(BF16)],
                axis=0,
            )
            act = jnp.dot(hidden[layer], columns, preferred_element_type=F32)
            act = act + bt[0:channels, layer + 1 : layer + 2]
            act = jnp.where(valid, jnp.maximum(act, 0.0), 0.0)
        acts.append(act.astype(BF16))
    pred = jnp.dot(ow[...], jnp.concatenate(acts, axis=0), preferred_element_type=F32) + out_bias[0]
    pred = pred.astype(BF16).astype(F32)
    odd = s % 2 == 1
    own = jnp.where(odd, filtered[3], filtered[2])
    alive = jnp.where(odd, live[3].astype(F32), live[2].astype(F32)) > 0.5
    pred = jnp.where(alive & valid, pred, 0.0)
    interference[...] = pltpu.roll(pred, span - LEAD, 1)[:, 0:samples].astype(BF16)
    difference = (own - pred).astype(BF16)
    zp[...] = jnp.zeros_like(zp)
    for w in range(samples // LANES):
        zp[8 : 8 + nodes, :] = contract_lanes(difference[:, w * LANES : w * LANES + window], tt2[...])
        acc = None
        for a in range(FN):
            v = zp[8 + a - FN // 2 : 8 + a - FN // 2 + nodes, a * LANES : (a + 1) * LANES]
            acc = v if acc is None else acc + v
        cleaned[:, w * LANES : (w + 1) * LANES] = jnp.where(alive, acc, 0.0).astype(BF16)


def local(
    records,
    live,
    dither,
    designature,
    first_weights,
    first_bias,
    hidden_weights,
    hidden_bias,
    out_weights,
    out_bias,
    shaping,
    shots,
    parts,
):
    _, nodes, samples = records.shape
    channels = first_weights.shape[0]
    total = samples * parts
    window = 2 * LANES
    windows = samples // LANES + 1
    span = windows * LANES
    s, t = lax.axis_index("shot"), lax.axis_index("tm")
    time_even, time_odd, partner, pair_even, pair_odd = exchanges(shots, parts)
    send = lambda x, pairs: lax.ppermute(x, AXES, pairs)

    info = jnp.stack([t, s]).astype(jnp.int32)
    vmem = pl.BlockSpec(memory_space=pltpu.VMEM)
    smem = pl.BlockSpec(memory_space=pltpu.SMEM)
    biases = jnp.concatenate([first_bias[None], hidden_bias], axis=0)
    tt1, tt2, w0, ow, bt = pl.pallas_call(
        prepare,
        out_shape=(
            jax.ShapeDtypeStruct((FN * LANES, window), BF16),
            jax.ShapeDtypeStruct((FN * LANES, window), BF16),
            jax.ShapeDtypeStruct((channels, 48), BF16),
            jax.ShapeDtypeStruct((nodes, nodes * channels), BF16),
            jax.ShapeDtypeStruct((LANES, 8), F32),
        ),
        in_specs=[smem] + [vmem] * 5,
        out_specs=(vmem,) * 5,
        scratch_shapes=[pltpu.VMEM((16, window), F32)],
        name="prepare",
    )(info, designature, shaping, first_weights, biases, out_weights[None])

    x = jnp.where(live[:, :, None] > 0, records, jnp.asarray(DEAD, BF16))
    a, b = send(x, time_even), send(x, time_odd)
    t_even = t % 2 == 0
    none = jnp.zeros_like(x)
    left = jnp.where(t == 0, none, jnp.where(t_even, b, a))
    right = jnp.where(t == parts - 1, none, jnp.where(t_even, a, b))
    x = jnp.concatenate([left, x, right], axis=2)
    y = send(x, partner)
    s_even = s % 2 == 0
    pair = jnp.concatenate([jnp.where(s_even, x, y), jnp.where(s_even, y, x)], axis=0)
    first, second = send(pair, pair_even), send(pair, pair_odd)

    rows = windows * 6 * nodes
    interference, cleaned = pl.pallas_call(
        functools.partial(deblend, total, shots),
        out_shape=(jax.ShapeDtypeStruct((nodes, samples), BF16),) * 2,
        in_specs=[smem] * 3 + [vmem] * 9,
        out_specs=(vmem,) * 2,
        scratch_shapes=[
            pltpu.VMEM((rows, window), BF16),
            pltpu.VMEM((windows * 6 * (nodes + 8) + 8, FN * LANES), F32),
            pltpu.VMEM((windows * nodes * 16, LANES), F32),
            pltpu.VMEM((nodes + 16, FN * LANES), F32),
        ],
        name="deblend",
    )(info, dither, out_bias, pair, first, second, tt1, tt2, w0, hidden_weights, bt, ow)
    return interference[None], cleaned[None]


def solution(mesh):
    shots, parts = mesh.shape["shot"], mesh.shape["tm"]
    in_specs = (P("shot", None, "tm"), P("shot", None), P(), P(), P(), P(), P(), P(), P(), P(), P())
    out_specs = (P("shot", None, "tm"), P("shot", None, "tm"))
    body = functools.partial(local, shots=shots, parts=parts)
    return jax.shard_map(body, mesh=mesh, in_specs=in_specs, out_specs=out_specs, check_vma=False)
```

time: 61.2 us -> 27.3 us (0.45)
  the two profiles are of different devices: /device:TPU:0 before, /device:TPU:10 now
where the time goes in v1:
time: 27.3 us; the launch traced here: 27 us
  Pallas kernels  12.9 us (47%)
  starting transfers between devices  4.7 us (17%)
  waiting for transfers between devices  3.61 us (13%)
  other arithmetic  2.59 us (9%)
  local copies, waits for them, and re-layouts  1.9 us (7%)
  between operations  1.36 us (5%)
    pallas_call x1, Pallas kernels, local(): pl.pallas_call(functools.partial(deblend, total, shots), out_shape=(jax.S...  10.7 us
    ppermute x5, starting transfers between devices, local(): send = lambda x, pairs: lax.ppermute(x, AXES, pairs)  4.7 us
    ppermute x5, waiting for transfers between devices, local(): send = lambda x, pairs: lax.ppermute(x, AXES, pairs)  3.61 us
    pallas_call x1, Pallas kernels, local(): pl.pallas_call(prepare, out_shape=(jax.ShapeDtypeStruct((FN * LANES, wind...  2.2 us
    unnamed x13, local copies, waits for them, and re-layouts  1.9 us
    select_n x1, other arithmetic, local(): x = jnp.where(live[:, :, None] > 0, records, jnp.asarray(DEAD, BF16))  0.76 us
    gt x1, other arithmetic, local(): x = jnp.where(live[:, :, None] > 0, records, jnp.asarray(DEAD, BF16))  0.66 us
    concatenate x1, other arithmetic, local(): biases = jnp.concatenate([first_bias[None], hidden_bias], axis=0)  0.59 us
  transfers between devices with their start and end apart: 5, of which 2 were waited for; matrix products, arithmetic and copies ran while one was open for 7% of the time, Pallas kernels for 8%

profile of v1, /device:TPU:10, one launch (start us, length us, event | category | flops | bytes accessed | tf_op | source)
XLA Modules:
  0.0 27.0 jit_solution(12934026661040536276)
XLA Ops:
  0.6 0.7 %compare_bitcast_fusion = pred[16]{0:T(512)(128)(4,1)S(1)} fusion(s32[1,16]{1,0:T(1,128)} %param.12), kind=kLoop, calls=%fused_computation.8 | loop fusion | flops 16 | bytes 80 | tf_op jit(solution)/shard_map/gt | solution.py:238
  1.3 0.8 %broadcast_select_fusion.2 = bf16[1,16,128]{2,1,0:T(8,128)(2,1)S(1)} fusion(bf16[1,16,128]{2,1,0:T(8,128)(2,1)} %param.11, pred[16]{0:T(512)(128)(4,1)S(1)} %compare_bitcast_fusion), kind=kLoop, calls=%fused_computation.6 | loop fusion | flops 2048 | bytes 8208 | tf_op jit(solution)/shard_map/jit(_where)/select_n | solution.py:238
  2.0 1.6 %collective-permute-start = (bf16[1,16,128]{2,1,0:T(8,128)(2,1)S(1)}, bf16[1,16,128]{2,1,0:T(8,128)(2,1)S(1)}, u32[]{:S(2)}, u32[]{:S(2)}) collective-permute-start(bf16[1,16,128]{2,1,0:T(8,128)(2,1)S(1)} %broadcast_select_fusion.2), channel_id=1, source_target_pairs={{0,4},{1,2},{2,1},{3,7},{4,0},{5,6},{6,5},{7,3},{8,12},{9,10},{10,... | collective-permute-start | bytes 12296 | tf_op jit(solution)/shard_map/ppermute | solution.py:217
  3.6 0.0 collective-permute-start.1
  3.6 2.0 %collective-permute-done = bf16[1,16,128]{2,1,0:T(8,128)(2,1)S(1)} collective-permute-done((bf16[1,16,128]{2,1,0:T(8,128)(2,1)S(1)}, bf16[1,16,128]{2,1,0:T(8,128)(2,1)S(1)}, u32[]{:S(2)}, u32[]{:S(2)}) %collective-permute-start) | collective-permute-done | bytes 4128 | tf_op jit(solution)/shard_map/ppermute | solution.py:217
  5.7 1.6 %collective-permute-done.1 = bf16[1,16,128]{2,1,0:T(8,128)(2,1)S(1)} collective-permute-done((bf16[1,16,128]{2,1,0:T(8,128)(2,1)S(1)}, bf16[1,16,128]{2,1,0:T(8,128)(2,1)S(1)}, u32[]{:S(2)}, u32[]{:S(2)}) %collective-permute-start.1) | collective-permute-done | bytes 4128 | tf_op jit(solution)/shard_map/ppermute | solution.py:217
  7.3 0.0 copy-start.5
  7.3 0.1 collective-permute-start.2
  7.3 0.6 %copy-done.4 = f32[3,64]{1,0:T(4,128)S(1)} copy-done((f32[3,64]{1,0:T(4,128)S(1)}, f32[3,64]{1,0:T(4,128)}, u32[]{:S(2)}) %copy-start.4) | copy-done | bytes 792
  7.9 0.6 %pad_maximum_fusion.2.biases = f32[4,64]{1,0:T(4,128)} fusion(f32[3,64]{1,0:T(4,128)S(1)} %copy-done.4, f32[1,64]{1,0:T(1,128)S(1)} %bitcast.9), kind=kLoop, calls=%fused_computation.7 | loop fusion | flops 256 | bytes 2048 | tf_op jit(solution)/shard_map/concatenate | solution.py:222
  8.5 0.0 collective-permute-done.2
  8.5 0.0 copy-start.3
  8.6 0.6 %collective-permute-start.3 = (bf16[2,16,384]{2,1,0:T(8,128)(2,1)S(1)}, bf16[2,16,384]{2,1,0:T(8,128)(2,1)S(1)}, u32[]{:S(2)}, u32[]{:S(2)}) collective-permute-start(bf16[2,16,384]{2,1,0:T(8,128)(2,1)S(1)} %pad_maximum_fusion.pair), channel_id=1, source_target_pairs={{0,8},{1,9},{2,10},{3,11},{4,12},{5,13},{6,14},{7,15},{8,0},{9,1},... | collective-permute-start | bytes 73736 | tf_op jit(solution)/shard_map/ppermute | solution.py:217
  9.2 2.4 %collective-permute-start.4 = (bf16[2,16,384]{2,1,0:T(8,128)(2,1)S(1)}, bf16[2,16,384]{2,1,0:T(8,128)(2,1)S(1)}, u32[]{:S(2)}, u32[]{:S(2)}) collective-permute-start(bf16[2,16,384]{2,1,0:T(8,128)(2,1)S(1)} %pad_maximum_fusion.pair), channel_id=1, source_target_pairs={{0,4},{1,5},{2,6},{3,7},{4,0},{5,1},{6,2},{7,3},{8,16},{9,17},{10,... | collective-permute-start | bytes 73736 | tf_op jit(solution)/shard_map/ppermute | solution.py:217
  11.6 0.6 %pad_add_fusion.info = s32[2]{0:T(128)} fusion(s32[1]{0:T(128)} %bitcast.1, s32[1]{0:T(128)} %bitcast), kind=kLoop, calls=%fused_computation.9 | loop fusion | flops 2 | bytes 16 | tf_op jit(solution)/shard_map/stack | solution.py:219
  12.2 0.0 copy-done.3
  12.2 0.7 %copy.13.first_weights = bf16[64,30]{1,0:T(8,128)(2,1)} copy(bf16[64,30]{0,1:T(8,128)(2,1)S(1)} %copy-done.3) | data formatting | bytes 7680 | tf_op args[4]
  13.5 2.2 %prepare.1 = (bf16[1152,256]{1,0:T(8,128)(2,1)}, bf16[1152,256]{1,0:T(8,128)(2,1)}, bf16[64,48]{1,0:T(8,128)(2,1)}, bf16[16,1024]{1,0:T(8,128)(2,1)}, f32[128,8]{1,0:T(8,128)}) custom-call(s32[2]{0:T(128)} %pad_add_fusion.info, bf16[9,33]{1,0:T(8,128)(2,1)} %designature.1, bf16[9,33]{1,0:T(8,128)(2,1)} %shaping.1, bf16[64,30]{1,0:T(8,128)(2,1)} %copy.13.first_weights, ...), custom_call_target="tpu_custom_call" | custom-call | tf_op jit(solution)/shard_map/prepare/pallas_call | solution.py:223
  15.7 0.0 collective-permute-done.3.first
  15.7 0.0 collective-permute-done.4.second
  15.8 0.0 copy-start.2
  15.8 0.6 %copy-done.1 = bf16[2,16,384]{2,1,0:T(8,128)(2,1)} copy-done((bf16[2,16,384]{2,1,0:T(8,128)(2,1)}, bf16[2,16,384]{2,1,0:T(8,128)(2,1)S(1)}, u32[]{:S(2)}) %copy-start.1) | copy-done | bytes 24600
  16.3 0.0 copy-done.2
  16.4 10.7 %deblend.1 = (bf16[16,128]{1,0:T(8,128)(2,1)}, bf16[16,128]{1,0:T(8,128)(2,1)}) custom-call(s32[2]{0:T(128)} %pad_add_fusion.info, s32[8]{0:T(128)} %dither.1, f32[1]{0:T(128)S(6)} %copy.14.out_bias, bf16[2,16,384]{2,1,0:T(8,128)(2,1)} %copy-done, bf16[2,16,384]{2,1,0:T(8,128)(2,1)} %copy-done.1, bf16[2,16,384]{2,1,0:T(8,128)(2,1)} %copy-done.2, ...), custom_call_target="tpu_custom_call" | custom-call | tf_op jit(solution)/shard_map/deblend/pallas_call | solution.py:251
  (9 shorter events, 0.0 us)
Async XLA Ops:
  2.0 3.6 %collective-permute-start = (bf16[1,16,128]{2,1,0:T(8,128)(2,1)S(1)}, bf16[1,16,128]{2,1,0:T(8,128)(2,1)S(1)}, u32[]{:S(2)}, u32[]{:S(2)}) collective-permute-start(bf16[1,16,128]{2,1,0:T(8,128)(2,1)S(1)} %broadcast_select_fusion.2), channel_id=1, source_target_pairs={{0,4},{1,2},{2,1},{3,7},{4,0},{5,6},{6,5},{7,3},{8,12},{9,10},{10,... | collective-permute-start | bytes 12296 | tf_op jit(solution)/shard_map/ppermute | solution.py:217
  3.6 3.6 %collective-permute-start.1 = (bf16[1,16,128]{2,1,0:T(8,128)(2,1)S(1)}, bf16[1,16,128]{2,1,0:T(8,128)(2,1)S(1)}, u32[]{:S(2)}, u32[]{:S(2)}) collective-permute-start(bf16[1,16,128]{2,1,0:T(8,128)(2,1)S(1)} %broadcast_select_fusion.2), channel_id=1, source_target_pairs={{0,1},{1,0},{2,3},{3,2},{4,5},{5,4},{6,7},{7,6},{8,9},{9,8},{10,11... | collective-permute-start | bytes 12296 | tf_op jit(solution)/shard_map/ppermute | solution.py:217
  7.2 0.7 %copy-start.4 = (f32[3,64]{1,0:T(4,128)S(1)}, f32[3,64]{1,0:T(4,128)}, u32[]{:S(2)}) copy-start(f32[3,64]{1,0:T(4,128)} %param.18) | copy-start | bytes 2308
  7.3 0.7 %copy-start.5 = (f32[64]{0:T(128)S(1)}, f32[64]{0:T(128)}, u32[]{:S(2)}) copy-start(f32[64]{0:T(128)} %param.16) | copy-start | bytes 772
  7.3 1.3 %collective-permute-start.2 = (bf16[1,16,384]{2,1,0:T(8,128)(2,1)S(1)}, bf16[1,16,384]{2,1,0:T(8,128)(2,1)S(1)}, u32[]{:S(2)}, u32[]{:S(2)}) collective-permute-start(bf16[1,16,384]{2,1,0:T(8,128)(2,1)S(1)} %pad_maximum_fusion.1), channel_id=1, source_target_pairs={{0,4},{1,5},{2,6},{3,7},{4,0},{5,1},{6,2},{7,3},{8,12},{9,13},{10,... | collective-permute-start | bytes 36872 | tf_op jit(solution)/shard_map/ppermute | solution.py:217
  8.5 3.6 %copy-start.3 = (bf16[64,30]{0,1:T(8,128)(2,1)S(1)}, bf16[64,30]{0,1:T(8,128)(2,1)}, u32[]{:S(2)}) copy-start(bf16[64,30]{0,1:T(8,128)(2,1)} %param.15) | copy-start | bytes 11524
  8.6 7.2 %copy-start = (bf16[2,16,384]{2,1,0:T(8,128)(2,1)}, bf16[2,16,384]{2,1,0:T(8,128)(2,1)S(1)}, u32[]{:S(2)}) copy-start(bf16[2,16,384]{2,1,0:T(8,128)(2,1)S(1)} %pad_maximum_fusion.pair) | copy-start | bytes 73732
  8.6 7.2 %collective-permute-start.3 = (bf16[2,16,384]{2,1,0:T(8,128)(2,1)S(1)}, bf16[2,16,384]{2,1,0:T(8,128)(2,1)S(1)}, u32[]{:S(2)}, u32[]{:S(2)}) collective-permute-start(bf16[2,16,384]{2,1,0:T(8,128)(2,1)S(1)} %pad_maximum_fusion.pair), channel_id=1, source_target_pairs={{0,8},{1,9},{2,10},{3,11},{4,12},{5,13},{6,14},{7,15},{8,0},{9,1},... | collective-permute-start | bytes 73736 | tf_op jit(solution)/shard_map/ppermute | solution.py:217
  9.2 6.6 %collective-permute-start.4 = (bf16[2,16,384]{2,1,0:T(8,128)(2,1)S(1)}, bf16[2,16,384]{2,1,0:T(8,128)(2,1)S(1)}, u32[]{:S(2)}, u32[]{:S(2)}) collective-permute-start(bf16[2,16,384]{2,1,0:T(8,128)(2,1)S(1)} %pad_maximum_fusion.pair), channel_id=1, source_target_pairs={{0,4},{1,5},{2,6},{3,7},{4,0},{5,1},{6,2},{7,3},{8,16},{9,17},{10,... | collective-permute-start | bytes 73736 | tf_op jit(solution)/shard_map/ppermute | solution.py:217
  15.7 0.6 %copy-start.1 = (bf16[2,16,384]{2,1,0:T(8,128)(2,1)}, bf16[2,16,384]{2,1,0:T(8,128)(2,1)S(1)}, u32[]{:S(2)}) copy-start(bf16[2,16,384]{2,1,0:T(8,128)(2,1)S(1)} %collective-permute-done.3.first) | copy-start | bytes 73732
  15.8 0.6 %copy-start.2 = (bf16[2,16,384]{2,1,0:T(8,128)(2,1)}, bf16[2,16,384]{2,1,0:T(8,128)(2,1)S(1)}, u32[]{:S(2)}) copy-start(bf16[2,16,384]{2,1,0:T(8,128)(2,1)S(1)} %collective-permute-done.4.second) | copy-start | bytes 73732

commit v2 on v1

--- a/solution.py
+++ b/solution.py
@@ -13,6 +13,7 @@
 SHOT_TAPS = 5
 DMAX = 32
 LANES = 128
+VMEM_LIMIT = 24 * 2**20
 LEAD = 32
 DEAD = 3e38
 LIMIT = 1e38
@@ -53,7 +54,7 @@
     return lax.dot_general(a, b, (((1,), (1,)), ((), ())), preferred_element_type=F32)
 
 
-def prepare(info, designature, shaping, first_weights, biases, out_weights, tt1, tt2, w0, ow, bt, pad):
+def prepare(designature, shaping, first_weights, first_bias, hidden_bias, out_weights, tt1, tt2, w0, ow, bt, pad):
     window = tt1.shape[1]
     for taps, offset, out in ((designature, window - LANES - LEAD - FT // 2, tt1), (shaping, LEAD - FT // 2, tt2)):
         pad[...] = jnp.zeros_like(pad)
@@ -62,14 +63,16 @@
             row = jnp.broadcast_to(pad[a : a + 1, :], (LANES, window))
             row = pltpu.roll(row, offset, 1, stride=1, stride_axis=0)
             out[a * LANES : (a + 1) * LANES, :] = row.astype(BF16)
-    parity = info[1] % 2
-    columns = first_weights.shape[1]
+    parity = lax.axis_index("shot") % 2
+    columns = first_weights.shape[0]
     f = lax.broadcasted_iota(jnp.int32, (columns, w0.shape[1]), 0)
     g = lax.broadcasted_iota(jnp.int32, (columns, w0.shape[1]), 1)
     c, a, k = f // (3 * SHOT_TAPS), (f // 3) % SHOT_TAPS, f % 3
     here = (g // 16 == k) & ((g // 8) % 2 == c) & (g % 8 == a + parity)
     select = jnp.where(here, 1.0, 0.0).astype(BF16)
-    w0[...] = jnp.dot(first_weights[...], select, preferred_element_type=F32).astype(BF16)
+    w0[...] = lax.dot_general(
+        first_weights[...], select, (((0,), (0,)), ((), ())), preferred_element_type=F32
+    ).astype(BF16)
     channels = out_weights.shape[1]
     nodes = ow.shape[0]
     row = out_weights[...].astype(F32)
@@ -79,14 +82,14 @@
         m = (lax.broadcasted_iota(jnp.int32, (nodes, LANES), 1) + i * LANES) // channels
         ow[:, i * LANES : (i + 1) * LANES] = jnp.where(m == n, jnp.broadcast_to(row, n.shape), 0.0).astype(BF16)
     pad[...] = jnp.zeros_like(pad)
-    pad[0 : biases.shape[0], 0:channels] = biases[...]
+    pad[0:1, 0:channels] = first_bias[...]
+    pad[1 : HID + 1, 0:channels] = hidden_bias[...]
     bt[...] = jnp.transpose(pad[0:8, 0:LANES])
 
 
 def deblend(
     total,
     shots,
-    info,
     dither,
     out_bias,
     pair,
@@ -110,7 +113,7 @@
     span = windows * LANES
     window = 2 * LANES
     channels = w0.shape[0]
-    t, s = info[0], info[1]
+    t, s = lax.axis_index("tm"), lax.axis_index("shot")
     chip = s // 2
     even = chip % 2 == 0
     lowest, highest = chip == 0, chip == shots // 2 - 1
@@ -162,17 +165,19 @@
     for n in range(nodes):
         columns = jnp.concatenate([v[16 * n : 16 * n + 16, :] for v in shifted], axis=0)
         act = jnp.dot(w0[...], columns, preferred_element_type=F32) + bt[0:channels, 0:1]
-        act = jnp.where(valid, jnp.maximum(act, 0.0), 0.0)
-        for layer in range(HID):
-            e = 2 ** (layer + 1)
+        acts.append(jnp.where(valid, jnp.maximum(act, 0.0), 0.0))
+    for layer in range(HID):
+        e = 2 ** (layer + 1)
+        bias = bt[0:channels, layer + 1 : layer + 2]
+        for n in range(nodes):
+            act = acts[n]
             columns = jnp.concatenate(
                 [pltpu.roll(act, e, 1).astype(BF16), act.astype(BF16), pltpu.roll(act, span - e, 1).astype(BF16)],
                 axis=0,
             )
-            act = jnp.dot(hidden[layer], columns, preferred_element_type=F32)
-            act = act + bt[0:channels, layer + 1 : layer + 2]
-            act = jnp.where(valid, jnp.maximum(act, 0.0), 0.0)
-        acts.append(act.astype(BF16))
+            act = jnp.dot(hidden[layer], columns, preferred_element_type=F32) + bias
+            acts[n] = jnp.where(valid, jnp.maximum(act, 0.0), 0.0)
+    acts = [act.astype(BF16) for act in acts]
     pred = jnp.dot(ow[...], jnp.concatenate(acts, axis=0), preferred_element_type=F32) + out_bias[0]
     pred = pred.astype(BF16).astype(F32)
     odd = s % 2 == 1
@@ -216,10 +221,8 @@
     time_even, time_odd, partner, pair_even, pair_odd = exchanges(shots, parts)
     send = lambda x, pairs: lax.ppermute(x, AXES, pairs)
 
-    info = jnp.stack([t, s]).astype(jnp.int32)
     vmem = pl.BlockSpec(memory_space=pltpu.VMEM)
     smem = pl.BlockSpec(memory_space=pltpu.SMEM)
-    biases = jnp.concatenate([first_bias[None], hidden_bias], axis=0)
     tt1, tt2, w0, ow, bt = pl.pallas_call(
         prepare,
         out_shape=(
@@ -229,19 +232,22 @@
             jax.ShapeDtypeStruct((nodes, nodes * channels), BF16),
             jax.ShapeDtypeStruct((LANES, 8), F32),
         ),
-        in_specs=[smem] + [vmem] * 5,
+        in_specs=[vmem] * 6,
         out_specs=(vmem,) * 5,
         scratch_shapes=[pltpu.VMEM((16, window), F32)],
+        compiler_params=pltpu.CompilerParams(vmem_limit_bytes=VMEM_LIMIT),
+        cost_estimate=pl.CostEstimate(flops=4 * 10**6, bytes_accessed=10**6, transcendentals=0),
         name="prepare",
-    )(info, designature, shaping, first_weights, biases, out_weights[None])
-
-    x = jnp.where(live[:, :, None] > 0, records, jnp.asarray(DEAD, BF16))
+    )(designature, shaping, first_weights.T, first_bias[None], hidden_bias, out_weights[None])
+
+    x = records
     a, b = send(x, time_even), send(x, time_odd)
     t_even = t % 2 == 0
     none = jnp.zeros_like(x)
     left = jnp.where(t == 0, none, jnp.where(t_even, b, a))
     right = jnp.where(t == parts - 1, none, jnp.where(t_even, a, b))
     x = jnp.concatenate([left, x, right], axis=2)
+    x = jnp.where(live[:, :, None] > 0, x, jnp.asarray(DEAD, BF16))
     y = send(x, partner)
     s_even = s % 2 == 0
     pair = jnp.concatenate([jnp.where(s_even, x, y), jnp.where(s_even, y, x)], axis=0)
@@ -251,7 +257,7 @@
     interference, cleaned = pl.pallas_call(
         functools.partial(deblend, total, shots),
         out_shape=(jax.ShapeDtypeStruct((nodes, samples), BF16),) * 2,
-        in_specs=[smem] * 3 + [vmem] * 9,
+        in_specs=[smem] * 2 + [vmem] * 9,
         out_specs=(vmem,) * 2,
         scratch_shapes=[
             pltpu.VMEM((rows, window), BF16),
@@ -259,8 +265,10 @@
             pltpu.VMEM((windows * nodes * 16, LANES), F32),
             pltpu.VMEM((nodes + 16, FN * LANES), F32),
         ],
+        compiler_params=pltpu.CompilerParams(vmem_limit_bytes=VMEM_LIMIT),
+        cost_estimate=pl.CostEstimate(flops=4 * 10**8, bytes_accessed=10**6, transcendentals=0),
         name="deblend",
-    )(info, dither, out_bias, pair, first, second, tt1, tt2, w0, hidden_weights, bt, ow)
+    )(dither, out_bias, pair, first, second, tt1, tt2, w0, hidden_weights, bt, ow)
     return interference[None], cleaned[None]
 
 

time: 27.3 us -> 18.8 us (0.69)
  the two profiles are of different devices: /device:TPU:10 before, /device:TPU:0 now
where the time goes in v2:
time: 18.8 us; the launch traced here: 18.6 us
  starting transfers between devices  7.75 us (41%)
  Pallas kernels  4.08 us (22%)
  waiting for transfers between devices  2.6 us (14%)
  local copies, waits for them, and re-layouts  1.98 us (11%)
  between operations  1.4 us (7%)
  other arithmetic  0.76 us (4%)
    ppermute x5, starting transfers between devices, local(): send = lambda x, pairs: lax.ppermute(x, AXES, pairs)  7.75 us
    pallas_call x1, Pallas kernels, local(): pl.pallas_call(functools.partial(deblend, total, shots), out_shape=(jax.S...  3.65 us
    ppermute x5, waiting for transfers between devices, local(): send = lambda x, pairs: lax.ppermute(x, AXES, pairs)  2.6 us
    unnamed x18, local copies, waits for them, and re-layouts  1.98 us
    gt x1, other arithmetic, local(): x = jnp.where(live[:, :, None] > 0, x, jnp.asarray(DEAD, BF16))  0.66 us
    pallas_call x1, Pallas kernels, local(): pl.pallas_call(prepare, out_shape=(jax.ShapeDtypeStruct((FN * LANES, wind...  0.43 us
  transfers between devices with their start and end apart: 5, of which 3 were waited for; matrix products, arithmetic and copies ran while one was open for 4% of the time, Pallas kernels for 2%

profile of v2, /device:TPU:0, one launch (start us, length us, event | category | flops | bytes accessed | tf_op | source)
XLA Modules:
  0.0 18.6 jit_solution(923537066331915095)
XLA Ops:
  0.6 0.6 %collective-permute-start = (bf16[1,16,128]{2,1,0:T(8,128)(2,1)}, bf16[1,16,128]{2,1,0:T(8,128)(2,1)S(1)}, u32[]{:S(2)}, u32[]{:S(2)}) collective-permute-start(bf16[1,16,128]{2,1,0:T(8,128)(2,1)} %param.11), channel_id=1, source_target_pairs={{0,4},{1,2},{2,1},{3,7},{4,0},{5,6},{6,5},{7,3},{8,12},{9,10},{10,... | collective-permute-start | bytes 12296 | tf_op jit(solution)/shard_map/ppermute | solution.py:222
  1.2 4.1 %collective-permute-start.1 = (bf16[1,16,128]{2,1,0:T(8,128)(2,1)}, bf16[1,16,128]{2,1,0:T(8,128)(2,1)S(1)}, u32[]{:S(2)}, u32[]{:S(2)}) collective-permute-start(bf16[1,16,128]{2,1,0:T(8,128)(2,1)} %param.11), channel_id=1, source_target_pairs={{0,1},{1,0},{2,3},{3,2},{4,5},{5,4},{6,7},{7,6},{8,9},{9,8},{10,11... | collective-permute-start | bytes 12296 | tf_op jit(solution)/shard_map/ppermute | solution.py:222
  5.3 0.7 %compare_bitcast_fusion = pred[16]{0:T(512)(128)(4,1)S(1)} fusion(s32[1,16]{1,0:T(1,128)} %param.12), kind=kLoop, calls=%fused_computation.6 | loop fusion | flops 16 | bytes 80 | tf_op jit(solution)/shard_map/gt | solution.py:250
  6.0 0.0 collective-permute-done
  6.0 1.2 %collective-permute-done.1 = bf16[1,16,128]{2,1,0:T(8,128)(2,1)S(1)} collective-permute-done((bf16[1,16,128]{2,1,0:T(8,128)(2,1)}, bf16[1,16,128]{2,1,0:T(8,128)(2,1)S(1)}, u32[]{:S(2)}, u32[]{:S(2)}) %collective-permute-start.1) | collective-permute-done | bytes 4128 | tf_op jit(solution)/shard_map/ppermute | solution.py:222
  7.2 0.7 %copy-done.8 = bf16[1,16,128]{2,1,0:T(8,128)(2,1)S(1)} copy-done((bf16[1,16,128]{2,1,0:T(8,128)(2,1)S(1)}, bf16[1,16,128]{2,1,0:T(8,128)(2,1)}, u32[]{:S(2)}) %copy-start.8) | copy-done | bytes 4120
  7.8 0.1 maximum_select_fusion
  7.9 0.0 collective-permute-start.2
  7.9 1.2 %collective-permute-done.2 = bf16[1,16,384]{2,1,0:T(8,128)(2,1)S(1)} collective-permute-done((bf16[1,16,384]{2,1,0:T(8,128)(2,1)S(1)}, bf16[1,16,384]{2,1,0:T(8,128)(2,1)S(1)}, u32[]{:S(2)}, u32[]{:S(2)}) %collective-permute-start.2) | collective-permute-done | bytes 12320 | tf_op jit(solution)/shard_map/ppermute | solution.py:222
  9.1 0.0 copy-start.2
  9.1 0.0 copy-start.1
  9.1 0.2 %collective-permute-start.4 = (bf16[2,16,384]{2,1,0:T(8,128)(2,1)S(1)}, bf16[2,16,384]{2,1,0:T(8,128)(2,1)S(1)}, u32[]{:S(2)}, u32[]{:S(2)}) collective-permute-start(bf16[2,16,384]{2,1,0:T(8,128)(2,1)S(1)} %pad_maximum_fusion.pair), channel_id=1, source_target_pairs={{0,4},{1,5},{2,6},{3,7},{4,0},{5,1},{6,2},{7,3},{8,16},{9,17},{10,... | collective-permute-start | bytes 73736 | tf_op jit(solution)/shard_map/ppermute | solution.py:222
  9.4 2.8 %collective-permute-start.3 = (bf16[2,16,384]{2,1,0:T(8,128)(2,1)S(1)}, bf16[2,16,384]{2,1,0:T(8,128)(2,1)S(1)}, u32[]{:S(2)}, u32[]{:S(2)}) collective-permute-start(bf16[2,16,384]{2,1,0:T(8,128)(2,1)S(1)} %pad_maximum_fusion.pair), channel_id=1, source_target_pairs={{0,8},{1,9},{2,10},{3,11},{4,12},{5,13},{6,14},{7,15},{8,0},{9,1},... | collective-permute-start | bytes 73736 | tf_op jit(solution)/shard_map/ppermute | solution.py:222
  12.8 0.0 copy-start.3
  12.9 0.0 copy-start.4
  12.9 0.0 copy-start.5
  12.9 0.0 copy-done
  12.9 0.0 copy-done.2
  12.9 0.6 %copy-done.3 = f32[3,64]{1,0:T(4,128)S(1)} copy-done((f32[3,64]{1,0:T(4,128)S(1)}, f32[3,64]{1,0:T(4,128)}, u32[]{:S(2)}) %copy-start.3) | copy-done | bytes 792
  13.5 0.4 %prepare.1 = (bf16[1152,256]{1,0:T(8,128)(2,1)S(1)}, bf16[1152,256]{1,0:T(8,128)(2,1)S(1)}, bf16[64,48]{1,0:T(8,128)(2,1)S(1)}, bf16[16,1024]{1,0:T(8,128)(2,1)S(1)}, f32[128,8]{1,0:T(8,128)S(1)}) custom-call(bf16[9,33]{1,0:T(8,128)(2,1)S(1)} %copy-done.1, bf16[9,33]{1,0:T(8,128)(2,1)S(1)} %copy-done.2, bf16[30,64]{1,0:T(8,128)(2,1)S(1)} %bitcast.7, ...), custom_call_target="tpu_custom_call" | custom-call | flops 4000000 | bytes 1000000 | tf_op jit(solution)/shard_map/prepare/pallas_call | solution.py:226
  14.0 0.0 collective-permute-done.4.second
  14.0 0.3 %collective-permute-done.3.first = bf16[2,16,384]{2,1,0:T(8,128)(2,1)S(1)} collective-permute-done((bf16[2,16,384]{2,1,0:T(8,128)(2,1)S(1)}, bf16[2,16,384]{2,1,0:T(8,128)(2,1)S(1)}, u32[]{:S(2)}, u32[]{:S(2)}) %collective-permute-start.3) | collective-permute-done | bytes 24608 | tf_op jit(solution)/shard_map/ppermute | solution.py:222
  14.3 0.7 %copy-done.7 = s32[8]{0:T(128)S(1)} copy-done((s32[8]{0:T(128)S(1)}, s32[8]{0:T(128)}, u32[]{:S(2)}) %copy-start.7) | copy-done | bytes 56
  14.9 3.6 %deblend.1 = (bf16[16,128]{1,0:T(8,128)(2,1)}, bf16[16,128]{1,0:T(8,128)(2,1)}) custom-call(s32[8]{0:T(128)S(1)} %copy-done.7, f32[1]{0:T(128)S(6)} %copy.13.out_bias, bf16[2,16,384]{2,1,0:T(8,128)(2,1)S(1)} %pad_maximum_fusion.pair, bf16[2,16,384]{2,1,0:T(8,128)(2,1)S(1)} %collective-permute-done.3.first, ...), custom_call_target="tpu_custom_call" | custom-call | flops 400000000 | bytes 1000000 | tf_op jit(solution)/shard_map/deblend/pallas_call | solution.py:257
  (11 shorter events, 0.0 us)
Async XLA Ops:
  0.6 5.4 %collective-permute-start = (bf16[1,16,128]{2,1,0:T(8,128)(2,1)}, bf16[1,16,128]{2,1,0:T(8,128)(2,1)S(1)}, u32[]{:S(2)}, u32[]{:S(2)}) collective-permute-start(bf16[1,16,128]{2,1,0:T(8,128)(2,1)} %param.11), channel_id=1, source_target_pairs={{0,4},{1,2},{2,1},{3,7},{4,0},{5,6},{6,5},{7,3},{8,12},{9,10},{10,... | collective-permute-start | bytes 12296 | tf_op jit(solution)/shard_map/ppermute | solution.py:222
  1.2 6.0 %collective-permute-start.1 = (bf16[1,16,128]{2,1,0:T(8,128)(2,1)}, bf16[1,16,128]{2,1,0:T(8,128)(2,1)S(1)}, u32[]{:S(2)}, u32[]{:S(2)}) collective-permute-start(bf16[1,16,128]{2,1,0:T(8,128)(2,1)} %param.11), channel_id=1, source_target_pairs={{0,1},{1,0},{2,3},{3,2},{4,5},{5,4},{6,7},{7,6},{8,9},{9,8},{10,11... | collective-permute-start | bytes 12296 | tf_op jit(solution)/shard_map/ppermute | solution.py:222
  7.2 0.7 %copy-start.8 = (bf16[1,16,128]{2,1,0:T(8,128)(2,1)S(1)}, bf16[1,16,128]{2,1,0:T(8,128)(2,1)}, u32[]{:S(2)}) copy-start(bf16[1,16,128]{2,1,0:T(8,128)(2,1)} %param.11) | copy-start | bytes 12292
  7.2 7.1 %copy-start.6 = (bf16[3,64,192]{2,1,0:T(8,128)(2,1)S(1)}, bf16[3,64,192]{2,1,0:T(8,128)(2,1)}, u32[]{:S(2)}) copy-start(bf16[3,64,192]{2,1,0:T(8,128)(2,1)} %hidden.1) | copy-start | bytes 221188
  7.9 1.2 %collective-permute-start.2 = (bf16[1,16,384]{2,1,0:T(8,128)(2,1)S(1)}, bf16[1,16,384]{2,1,0:T(8,128)(2,1)S(1)}, u32[]{:S(2)}, u32[]{:S(2)}) collective-permute-start(bf16[1,16,384]{2,1,0:T(8,128)(2,1)S(1)} %maximum_select_fusion), channel_id=1, source_target_pairs={{0,4},{1,5},{2,6},{3,7},{4,0},{5,1},{6,2},{7,3},{8,12},{9,13},{10,... | collective-permute-start | bytes 36872 | tf_op jit(solution)/shard_map/ppermute | solution.py:222
  9.1 3.8 %copy-start = (bf16[64,30]{0,1:T(8,128)(2,1)S(1)}, bf16[64,30]{0,1:T(8,128)(2,1)}, u32[]{:S(2)}) copy-start(bf16[64,30]{0,1:T(8,128)(2,1)} %param.15) | copy-start | bytes 11524
  9.1 3.8 %copy-start.2 = (bf16[9,33]{1,0:T(8,128)(2,1)S(1)}, bf16[9,33]{1,0:T(8,128)(2,1)}, u32[]{:S(2)}) copy-start(bf16[9,33]{1,0:T(8,128)(2,1)} %shaping.1) | copy-start | bytes 1786
  9.1 3.8 %copy-start.1 = (bf16[9,33]{1,0:T(8,128)(2,1)S(1)}, bf16[9,33]{1,0:T(8,128)(2,1)}, u32[]{:S(2)}) copy-start(bf16[9,33]{1,0:T(8,128)(2,1)} %designature.1) | copy-start | bytes 1786
  9.1 4.8 %collective-permute-start.4 = (bf16[2,16,384]{2,1,0:T(8,128)(2,1)S(1)}, bf16[2,16,384]{2,1,0:T(8,128)(2,1)S(1)}, u32[]{:S(2)}, u32[]{:S(2)}) collective-permute-start(bf16[2,16,384]{2,1,0:T(8,128)(2,1)S(1)} %pad_maximum_fusion.pair), channel_id=1, source_target_pairs={{0,4},{1,5},{2,6},{3,7},{4,0},{5,1},{6,2},{7,3},{8,16},{9,17},{10,... | collective-permute-start | bytes 73736 | tf_op jit(solution)/shard_map/ppermute | solution.py:222
  9.4 4.9 %collective-permute-start.3 = (bf16[2,16,384]{2,1,0:T(8,128)(2,1)S(1)}, bf16[2,16,384]{2,1,0:T(8,128)(2,1)S(1)}, u32[]{:S(2)}, u32[]{:S(2)}) collective-permute-start(bf16[2,16,384]{2,1,0:T(8,128)(2,1)S(1)} %pad_maximum_fusion.pair), channel_id=1, source_target_pairs={{0,8},{1,9},{2,10},{3,11},{4,12},{5,13},{6,14},{7,15},{8,0},{9,1},... | collective-permute-start | bytes 73736 | tf_op jit(solution)/shard_map/ppermute | solution.py:222
  12.8 0.7 %copy-start.3 = (f32[3,64]{1,0:T(4,128)S(1)}, f32[3,64]{1,0:T(4,128)}, u32[]{:S(2)}) copy-start(f32[3,64]{1,0:T(4,128)} %hidden_bias.1) | copy-start | bytes 2308
  12.9 0.7 %copy-start.4 = (f32[64]{0:T(128)S(1)}, f32[64]{0:T(128)}, u32[]{:S(2)}) copy-start(f32[64]{0:T(128)} %param.16) | copy-start | bytes 772
  12.9 0.7 %copy-start.5 = (bf16[64]{0:T(256)(128)(2,1)S(1)}, bf16[64]{0:T(256)(128)(2,1)}, u32[]{:S(2)}) copy-start(bf16[64]{0:T(256)(128)(2,1)} %param.19) | copy-start | bytes 388
  14.3 0.7 %copy-start.7 = (s32[8]{0:T(128)S(1)}, s32[8]{0:T(128)}, u32[]{:S(2)}) copy-start(s32[8]{0:T(128)} %dither.1) | copy-start | bytes 100

commit v3 on v2

v3 whole, which is shorter than its diff:
```python
import functools

import jax
import jax.numpy as jnp
from jax import lax
from jax.experimental import pallas as pl
from jax.experimental.pallas import tpu as pltpu
from jax.sharding import PartitionSpec as P

HID = 3
FN = 9
FT = 33
SHOT_TAPS = 5
DMAX = 32
LANES = 128
VMEM_LIMIT = 24 * 2**20
LEAD = 32
BEFORE = LEAD + FT // 2
DEAD = 3e38
LIMIT = 1e38
OFF = 1e30
F32 = jnp.float32
BF16 = jnp.bfloat16
AXES = ("shot", "tm")


def partners(shots, parts, rule):
    out = []
    for s in range(shots):
        for t in range(parts):
            a, b = rule(s, t)
            out.append((s * parts + t, a * parts + b))
    return out


def exchanges(shots, parts):
    def time_odd(s, t):
        o = ((t + 1) ^ 1) - 1
        return (s, o) if 0 <= o < parts else (s ^ 1, t)

    def pair_odd(s, t):
        o = ((s // 2 + 1) ^ 1) - 1
        return (2 * o + s % 2, t) if 0 <= o < shots // 2 else (s ^ 1, t)

    rules = (
        lambda s, t: (s, t ^ 1),
        time_odd,
        lambda s, t: (s ^ 1, t),
        lambda s, t: (s ^ 2, t),
        pair_odd,
    )
    return [partners(shots, parts, rule) for rule in rules]


def contract_lanes(a, b):
    return lax.dot_general(a, b, (((1,), (1,)), ((), ())), preferred_element_type=F32)


def extras(column, lanes, start):
    high = column.astype(BF16).astype(F32)
    middle = (column - high).astype(BF16).astype(F32)
    low = column - high - middle
    out = jnp.where(lanes == start, high, 0.0)
    out = jnp.where(lanes == start + 1, middle, out)
    out = jnp.where(lanes == start + 2, low, out)
    return jnp.where(lanes == start + 3, -OFF, out)


def prepare(
    dither, designature, shaping, first_weights, first_bias, hidden_weights, hidden_bias, out_weights, out_bias,
    tt1, tt2, w0, wh, ow, small, pad
):
    window = tt1.shape[1]
    for taps, offset, out in ((designature, 0, tt1), (shaping, LEAD - FT // 2, tt2)):
        pad[...] = jnp.zeros_like(pad)
        pad[0:FN, 0:FT] = taps[...].astype(F32)
        for a in range(FN):
            row = jnp.broadcast_to(pad[a : a + 1, :], (LANES, window))
            row = pltpu.roll(row, offset, 1, stride=1, stride_axis=0)
            out[a * LANES : (a + 1) * LANES, :] = row.astype(BF16)
    channels = out_weights.shape[1]
    pad[...] = jnp.zeros_like(pad)
    pad[0:1, 0:channels] = first_bias[...]
    pad[1 : HID + 1, 0:channels] = hidden_bias[...]
    bias = jnp.transpose(pad[0:8, 0:LANES])[0:channels, :]
    parity = lax.axis_index("shot") % 2
    columns = first_weights.shape[0]
    f = lax.broadcasted_iota(jnp.int32, (columns, w0.shape[1]), 0)
    g = lax.broadcasted_iota(jnp.int32, (columns, w0.shape[1]), 1)
    c, a, k = f // (3 * SHOT_TAPS), (f // 3) % SHOT_TAPS, f % 3
    here = (g // 16 == k) & ((g // 8) % 2 == c) & (g % 8 == a + parity)
    select = jnp.where(here, 1.0, 0.0).astype(BF16)
    value = lax.dot_general(first_weights[...], select, (((0,), (0,)), ((), ())), preferred_element_type=F32)
    lanes = lax.broadcasted_iota(jnp.int32, w0.shape, 1)
    w0[...] = (value + extras(bias[:, 0:1], lanes, 48)).astype(BF16)
    taps = hidden_weights.shape[2]
    unit = jnp.where(
        lax.broadcasted_iota(jnp.int32, (taps, wh.shape[2]), 0)
        == lax.broadcasted_iota(jnp.int32, (taps, wh.shape[2]), 1),
        1.0,
        0.0,
    ).astype(BF16)
    lanes = lax.broadcasted_iota(jnp.int32, wh.shape[1:], 1)
    for layer in range(HID):
        value = jnp.dot(hidden_weights[layer], unit, preferred_element_type=F32)
        wh[layer] = (value + extras(bias[:, layer + 1 : layer + 2], lanes, taps)).astype(BF16)
    nodes = ow.shape[0]
    row = out_weights[...].astype(F32)
    row = jnp.concatenate([row] * (LANES // channels), axis=1)
    n = lax.broadcasted_iota(jnp.int32, (nodes, LANES), 0)
    for i in range(ow.shape[1] // LANES):
        m = (lax.broadcasted_iota(jnp.int32, (nodes, LANES), 1) + i * LANES) // channels
        ow[:, i * LANES : (i + 1) * LANES] = jnp.where(m == n, jnp.broadcast_to(row, n.shape), 0.0).astype(BF16)
    pad[0:1, 0 : dither.shape[1]] = dither[...].astype(F32)
    small[0:1, :] = jnp.broadcast_to(out_bias[...], (1, LANES))
    small[1:2, :] = pad[0:1, 0:LANES]


def moved(tiles, by):
    n = len(tiles)
    lanes = lax.broadcasted_iota(jnp.int32, tiles[0].shape, 1)
    turned = [pltpu.roll(v, by % LANES, 1) for v in tiles]
    if by > 0:
        return [turned[0]] + [jnp.where(lanes < by, turned[i - 1], turned[i]) for i in range(1, n)]
    return [jnp.where(lanes >= LANES + by, turned[i + 1], turned[i]) for i in range(n - 1)] + [turned[n - 1]]


def taps_of(tiles, by):
    up, down = moved(tiles, by), moved(tiles, -by)
    return [jnp.concatenate(v, axis=1) for v in (up, tiles, down)]


def deblend(
    total,
    shots,
    pair,
    first,
    second,
    tt1,
    tt2,
    w0,
    wh,
    ow,
    small,
    interference,
    cleaned,
    xn,
    gs,
    zp,
):
    nodes, samples = interference.shape
    windows = samples // LANES + 1
    span = windows * LANES
    window = 2 * LANES
    channels = w0.shape[0]
    rows = nodes * 8
    t, s = lax.axis_index("tm"), lax.axis_index("shot")
    chip = s // 2
    even = chip % 2 == 0
    lowest, highest = chip == 0, chip == shots // 2 - 1
    zero = jnp.zeros((nodes, LANES), F32)
    own_live = []
    for j in range(8):
        if 2 <= j < 4:
            x = pair[j - 2].astype(F32)
            own_live.append(x[:, BEFORE : BEFORE + 1])
        elif j < 6:
            p, q = (second, first) if j < 2 else (first, second)
            x = jnp.where(even, p[j % 2].astype(F32), q[j % 2].astype(F32))
            x = jnp.where(lowest if j < 2 else highest, 0.0, x)
        for w in range(windows):
            xn[pl.ds(w * rows + j, nodes, stride=8), :] = zero if j >= 6 else x[:, w * LANES : (w + 1) * LANES]
            if j >= 6:
                gs[pl.ds(w * rows * 2 + j, nodes, stride=16), :] = zero
                gs[pl.ds(w * rows * 2 + j + 8, nodes, stride=16), :] = zero
    x = [xn[w * rows : (w + 1) * rows, :] for w in range(windows)]
    live = x[BEFORE // LANES][:, BEFORE % LANES : BEFORE % LANES + 1] < LIMIT
    x = [jnp.where(v < LIMIT, v, 0.0).astype(BF16) for v in x] + [jnp.zeros((rows, LANES), BF16)]
    x = jnp.concatenate([jnp.concatenate(x[w : w + 2], axis=1) for w in range(windows)], axis=0)
    sums = [[None] * nodes for _ in range(windows)]
    for a0 in range(0, FN, 2):
        count = min(2, FN - a0)
        y = contract_lanes(x, tt1[a0 * LANES : (a0 + count) * LANES, :])
        for a in range(a0, a0 + count):
            for w in range(windows):
                for n in range(nodes):
                    m = n + a - FN // 2
                    if 0 <= m < nodes:
                        row = w * rows + m * 8
                        v = y[row : row + 8, (a - a0) * LANES : (a - a0 + 1) * LANES]
                        sums[w][n] = v if sums[w][n] is None else sums[w][n] + v
    position = t * samples - LEAD + lax.broadcasted_iota(jnp.int32, (1, span), 1)
    valid = (position >= 0) & (position < total)
    for w in range(windows):
        inside = valid[:, w * LANES : (w + 1) * LANES]
        for n in range(nodes):
            f = jnp.where(live[n * 8 : n * 8 + 8, :] & inside, sums[w][n], 0.0)
            gs[(w * nodes + n) * 16 : (w * nodes + n) * 16 + 8, :] = f.astype(BF16).astype(F32)
    delays = small[1:2, :]
    lane = lax.broadcasted_iota(jnp.int32, (1, LANES), 1)
    own = []
    for j in range(6):
        f = jnp.concatenate([gs[pl.ds(w * rows * 2 + j, nodes, stride=16), :] for w in range(windows)], axis=1)
        if 2 <= j < 4:
            own.append(f)
        shot = jnp.clip(2 * chip - 2 + j, 0, shots - 1)
        delay = jnp.sum(jnp.where(lane == shot, delays, 0.0)).astype(jnp.int32)
        r = jnp.where(valid, pltpu.roll(f, span - delay, 1), 0.0)
        for w in range(windows):
            gs[pl.ds(w * rows * 2 + j + 8, nodes, stride=16), :] = r[:, w * LANES : (w + 1) * LANES]
    row = lax.broadcasted_iota(jnp.int32, (16, span), 0)
    extra = jnp.where(row < 3, 1.0, jnp.where((row == 3) & ~valid, 1.0, 0.0)).astype(BF16)
    acts = []
    for n in range(nodes):
        tiles = [gs[(w * nodes + n) * 16 : (w * nodes + n + 1) * 16, :].astype(BF16) for w in range(windows)]
        columns = jnp.concatenate(taps_of(tiles, 1) + [extra], axis=0)
        act = jnp.dot(w0[...], columns, preferred_element_type=F32)
        acts.append(jnp.maximum(act.astype(BF16), 0.0))
    for layer in range(HID):
        for n in range(nodes):
            tiles = [acts[n][:, w * LANES : (w + 1) * LANES] for w in range(windows)]
            columns = jnp.concatenate(taps_of(tiles, 2 ** (layer + 1)) + [extra], axis=0)
            act = jnp.dot(wh[layer], columns, preferred_element_type=F32)
            acts[n] = jnp.maximum(act.astype(BF16), 0.0)
    pred = jnp.dot(ow[...], jnp.concatenate(acts, axis=0), preferred_element_type=F32) + small[0:1, 0:1]
    pred = pred.astype(BF16).astype(F32)
    odd = s % 2 == 1
    own = jnp.where(odd, own[1], own[0])
    alive = jnp.where(odd, own_live[1], own_live[0]) < LIMIT
    pred = jnp.where(alive & valid, pred, 0.0)
    interference[...] = pltpu.roll(pred, span - LEAD, 1)[:, 0:samples].astype(BF16)
    difference = (own - pred).astype(BF16)
    zp[0:8, :] = jnp.zeros((8, zp.shape[1]), F32)
    zp[nodes + 8 : nodes + 16, :] = jnp.zeros((8, zp.shape[1]), F32)
    for w in range(samples // LANES):
        zp[8 : 8 + nodes, :] = contract_lanes(difference[:, w * LANES : w * LANES + window], tt2[...])
        acc = None
        for a in range(FN):
            v = zp[8 + a - FN // 2 : 8 + a - FN // 2 + nodes, a * LANES : (a + 1) * LANES]
            acc = v if acc is None else acc + v
        cleaned[:, w * LANES : (w + 1) * LANES] = jnp.where(alive, acc, 0.0).astype(BF16)


def local(
    records,
    live,
    dither,
    designature,
    first_weights,
    first_bias,
    hidden_weights,
    hidden_bias,
    out_weights,
    out_bias,
    shaping,
    shots,
    parts,
):
    _, nodes, samples = records.shape
    channels = first_weights.shape[0]
    total = samples * parts
    window = 2 * LANES
    windows = samples // LANES + 1
    span = windows * LANES
    frame = span
    s, t = lax.axis_index("shot"), lax.axis_index("tm")
    time_even, time_odd, partner, pair_even, pair_odd = exchanges(shots, parts)
    send = lambda x, pairs: lax.ppermute(x, AXES, pairs)

    vmem = pl.BlockSpec(memory_space=pltpu.VMEM)
    tt1, tt2, w0, wh, ow, small = pl.pallas_call(
        prepare,
        out_shape=(
            jax.ShapeDtypeStruct((FN * LANES, window), BF16),
            jax.ShapeDtypeStruct((FN * LANES, window), BF16),
            jax.ShapeDtypeStruct((channels, 64), BF16),
            jax.ShapeDtypeStruct((HID, channels, 3 * channels + 16), BF16),
            jax.ShapeDtypeStruct((nodes, nodes * channels), BF16),
            jax.ShapeDtypeStruct((8, LANES), F32),
        ),
        in_specs=[vmem] * 9,
        out_specs=(vmem,) * 6,
        scratch_shapes=[pltpu.VMEM((16, window), F32)],
        compiler_params=pltpu.CompilerParams(vmem_limit_bytes=VMEM_LIMIT),
        cost_estimate=pl.CostEstimate(flops=4 * 10**6, bytes_accessed=10**6, transcendentals=0),
        name="prepare",
    )(
        dither[None],
        designature,
        shaping,
        first_weights.T,
        first_bias[None],
        hidden_weights,
        hidden_bias,
        out_weights[None],
        out_bias[None],
    )

    keep = live[:, :, None] > 0
    dead = jnp.asarray(DEAD, BF16)
    a, b = send(records, time_even), send(records, time_odd)
    mine = lax.optimization_barrier(jnp.where(keep, records, dead))
    t_even = t % 2 == 0
    left = jnp.where(t_even, b, a)[:, :, samples - BEFORE :]
    right = jnp.where(t_even, a, b)[:, :, : frame - BEFORE - samples]
    left = jnp.where(t == 0, jnp.zeros_like(left), left)
    right = jnp.where(t == parts - 1, jnp.zeros_like(right), right)
    x = jnp.concatenate([jnp.where(keep, left, dead), mine, jnp.where(keep, right, dead)], axis=2)
    y = send(x, partner)
    s_even = s % 2 == 0
    pair = jnp.concatenate([jnp.where(s_even, x, y), jnp.where(s_even, y, x)], axis=0)
    first, second = send(pair, pair_even), send(pair, pair_odd)

    interference, cleaned = pl.pallas_call(
        functools.partial(deblend, total, shots),
        out_shape=(jax.ShapeDtypeStruct((nodes, samples), BF16),) * 2,
        in_specs=[vmem] * 9,
        out_specs=(vmem,) * 2,
        scratch_shapes=[
            pltpu.VMEM((windows * nodes * 8, LANES), F32),
            pltpu.VMEM((windows * nodes * 16, LANES), F32),
            pltpu.VMEM((nodes + 16, FN * LANES), F32),
        ],
        compiler_params=pltpu.CompilerParams(vmem_limit_bytes=VMEM_LIMIT),
        cost_estimate=pl.CostEstimate(flops=4 * 10**8, bytes_accessed=10**6, transcendentals=0),
        name="deblend",
    )(pair, first, second, tt1, tt2, w0, wh, ow, small)
    return interference[None], cleaned[None]


def solution(mesh):
    shots, parts = mesh.shape["shot"], mesh.shape["tm"]
    in_specs = (P("shot", None, "tm"), P("shot", None), P(), P(), P(), P(), P(), P(), P(), P(), P())
    out_specs = (P("shot", None, "tm"), P("shot", None, "tm"))
    body = functools.partial(local, shots=shots, parts=parts)
    return jax.shard_map(body, mesh=mesh, in_specs=in_specs, out_specs=out_specs, check_vma=False)
```

time: 18.8 us -> 16.7 us (0.89)
  local copies, waits for them, and re-layouts: 1.98 us -> 0.64 us
  waiting for transfers between devices: 2.6 us -> 1.58 us
  other arithmetic: 0.76 us -> 1.73 us
  Pallas kernels: 4.08 us -> 3.38 us
    unnamed x18 -> x16, local copies, waits for them, and re-layouts: 1.98 us -> 0.64 us
    ppermute x5, waiting for transfers between devices: 2.6 us -> 1.58 us  [local(): send = lambda x, pairs: lax.ppermute(x, AXES, pairs)]
    select_n x2 -> x3, other arithmetic: 0.08 us -> 0.91 us  [the longest x1 0.76 us: local(): mine = lax.optimization_barrier(jnp.where(keep, records, dead))]
    pallas_call x1, Pallas kernels: 3.65 us -> 2.88 us  [local(): pl.pallas_call(functools.partial(deblend, total, shots), out_shape=(jax.S...]
  transfers between devices with their start and end apart: 5 -> 5, of which waited for: 3 -> 2; matrix products, arithmetic and copies ran while one was open for 4% -> 9% of each run, Pallas kernels for 2% -> 3%
where the time goes in v3:
time: 16.7 us; the launch traced here: 16.5 us
  starting transfers between devices  7.75 us (46%)
  Pallas kernels  3.38 us (20%)
  other arithmetic  1.73 us (10%)
  waiting for transfers between devices  1.58 us (9%)
  between operations  1.42 us (9%)
  local copies, waits for them, and re-layouts  0.64 us (4%)
    ppermute x5, starting transfers between devices, local(): send = lambda x, pairs: lax.ppermute(x, AXES, pairs)  7.75 us
    pallas_call x1, Pallas kernels, local(): pl.pallas_call(functools.partial(deblend, total, shots), out_shape=(jax.S...  2.88 us
    ppermute x5, waiting for transfers between devices, local(): send = lambda x, pairs: lax.ppermute(x, AXES, pairs)  1.58 us
    select_n x1, other arithmetic, local(): mine = lax.optimization_barrier(jnp.where(keep, records, dead))  0.76 us
    gt x1, other arithmetic, local(): keep = live[:, :, None] > 0  0.66 us
    unnamed x16, local copies, waits for them, and re-layouts  0.64 us
    pallas_call x1, Pallas kernels, local(): pl.pallas_call(prepare, out_shape=(jax.ShapeDtypeStruct((FN * LANES, wind...  0.5 us
  transfers between devices with their start and end apart: 5, of which 2 were waited for; matrix products, arithmetic and copies ran while one was open for 9% of the time, Pallas kernels for 3%

profile of v3, /device:TPU:0, one launch (start us, length us, event | category | flops | bytes accessed | tf_op | source)
XLA Modules:
  0.0 16.5 jit_solution(10927756150810102161)
XLA Ops:
  0.6 0.6 %collective-permute-start = (bf16[1,16,128]{2,1,0:T(8,128)(2,1)}, bf16[1,16,128]{2,1,0:T(8,128)(2,1)S(1)}, u32[]{:S(2)}, u32[]{:S(2)}) collective-permute-start(bf16[1,16,128]{2,1,0:T(8,128)(2,1)} %param.11), channel_id=1, source_target_pairs={{0,4},{1,2},{2,1},{3,7},{4,0},{5,6},{6,5},{7,3},{8,12},{9,10},{10,... | collective-permute-start | bytes 12296 | tf_op jit(solution)/shard_map/ppermute | solution.py:268
  1.2 4.1 %collective-permute-start.1 = (bf16[1,16,128]{2,1,0:T(8,128)(2,1)}, bf16[1,16,128]{2,1,0:T(8,128)(2,1)S(1)}, u32[]{:S(2)}, u32[]{:S(2)}) collective-permute-start(bf16[1,16,128]{2,1,0:T(8,128)(2,1)} %param.11), channel_id=1, source_target_pairs={{0,1},{1,0},{2,3},{3,2},{4,5},{5,4},{6,7},{7,6},{8,9},{9,8},{10,11... | collective-permute-start | bytes 12296 | tf_op jit(solution)/shard_map/ppermute | solution.py:268
  5.3 0.7 %compare_bitcast_fusion = pred[16]{0:T(512)(128)(4,1)S(1)} fusion(s32[1,16]{1,0:T(1,128)} %param.12), kind=kLoop, calls=%fused_computation.11 | loop fusion | flops 16 | bytes 80 | tf_op jit(solution)/shard_map/gt | solution.py:299
  6.0 0.8 %broadcast_select_fusion.2 = bf16[1,16,128]{2,1,0:T(8,128)(2,1)S(1)} fusion(bf16[1,16,128]{2,1,0:T(8,128)(2,1)} %param.11, pred[16]{0:T(512)(128)(4,1)S(1)} %compare_bitcast_fusion), kind=kLoop, calls=%fused_computation.10 | loop fusion | flops 2048 | bytes 8208 | tf_op jit(solution)/shard_map/jit(_where)/select_n | solution.py:302
  6.7 0.0 collective-permute-done
  6.8 0.4 %collective-permute-done.1 = bf16[1,16,128]{2,1,0:T(8,128)(2,1)S(1)} collective-permute-done((bf16[1,16,128]{2,1,0:T(8,128)(2,1)}, bf16[1,16,128]{2,1,0:T(8,128)(2,1)S(1)}, u32[]{:S(2)}, u32[]{:S(2)}) %collective-permute-start.1) | collective-permute-done | bytes 4128 | tf_op jit(solution)/shard_map/ppermute | solution.py:268
  7.2 0.1 fusion.1
  7.2 0.1 fusion.3
  7.3 0.1 pad_maximum_fusion.1
  7.4 0.0 collective-permute-start.2
  7.4 1.1 %collective-permute-done.2 = bf16[1,16,256]{2,1,0:T(8,128)(2,1)S(1)} collective-permute-done((bf16[1,16,256]{2,1,0:T(8,128)(2,1)S(1)}, bf16[1,16,256]{2,1,0:T(8,128)(2,1)S(1)}, u32[]{:S(2)}, u32[]{:S(2)}) %collective-permute-start.2) | collective-permute-done | bytes 8224 | tf_op jit(solution)/shard_map/ppermute | solution.py:268
  8.6 0.1 broadcast_select_fusion.1
  8.6 0.0 copy-start.7
  8.7 0.0 copy-start.1
  8.7 0.2 %collective-permute-start.4 = (bf16[2,16,256]{2,1,0:T(8,128)(2,1)S(1)}, bf16[2,16,256]{2,1,0:T(8,128)(2,1)S(1)}, u32[]{:S(2)}, u32[]{:S(2)}) collective-permute-start(bf16[2,16,256]{2,1,0:T(8,128)(2,1)S(1)} %pad_maximum_fusion.pair), channel_id=1, source_target_pairs={{0,4},{1,5},{2,6},{3,7},{4,0},{5,1},{6,2},{7,3},{8,16},{9,17},{10,... | collective-permute-start | bytes 49160 | tf_op jit(solution)/shard_map/ppermute | solution.py:268
  8.9 2.8 %collective-permute-start.3 = (bf16[2,16,256]{2,1,0:T(8,128)(2,1)S(1)}, bf16[2,16,256]{2,1,0:T(8,128)(2,1)S(1)}, u32[]{:S(2)}, u32[]{:S(2)}) collective-permute-start(bf16[2,16,256]{2,1,0:T(8,128)(2,1)S(1)} %pad_maximum_fusion.pair), channel_id=1, source_target_pairs={{0,8},{1,9},{2,10},{3,11},{4,12},{5,13},{6,14},{7,15},{8,0},{9,1},... | collective-permute-start | bytes 49160 | tf_op jit(solution)/shard_map/ppermute | solution.py:268
  12.4 0.0 copy-start.4
  12.4 0.0 copy-start.5
  12.4 0.0 copy-start.6
  12.5 0.6 %copy-done.4 = f32[3,64]{1,0:T(4,128)S(1)} copy-done((f32[3,64]{1,0:T(4,128)S(1)}, f32[3,64]{1,0:T(4,128)}, u32[]{:S(2)}) %copy-start.4) | copy-done | bytes 792
  13.1 0.5 %prepare.1 = (bf16[1152,256]{1,0:T(8,128)(2,1)S(1)}, bf16[1152,256]{1,0:T(8,128)(2,1)S(1)}, bf16[64,64]{1,0:T(8,128)(2,1)S(1)}, bf16[3,64,208]{2,1,0:T(8,128)(2,...) custom-call(s32[1,8]{1,0:T(1,128)S(1)} %bitcast.11, bf16[9,33]{1,0:T(8,128)(2,1)S(1)} %copy-done.2, ...), custom_call_target="tpu_custom_call" | custom-call | flops 4000000 | bytes 1000000 | tf_op jit(solution)/shard_map/prepare/pallas_call | solution.py:271
  13.6 0.0 collective-permute-done.4.second
  13.6 0.0 collective-permute-done.3.first
  13.6 2.9 %deblend.1 = (bf16[16,128]{1,0:T(8,128)(2,1)}, bf16[16,128]{1,0:T(8,128)(2,1)}) custom-call(bf16[2,16,256]{2,1,0:T(8,128)(2,1)S(1)} %pad_maximum_fusion.pair, bf16[2,16,256]{2,1,0:T(8,128)(2,1)S(1)} %collective-permute-done.3.first, bf16[2,16,256]{2,1,0:T(8,128)(2,1)S(1)} %collective-permute-done.4.second, bf16[1152,256]{1,0:T(8,128)(2,1)S(1)} %get-tuple-element.10.tt1, ...), custom_call_target="tpu_custom_call" | custom-call | flops 400000000 | bytes 1000000 | tf_op jit(solution)/shard_map/deblend/pallas_call | solution.py:314
  (11 shorter events, 0.0 us)
Async XLA Ops:
  0.6 6.1 %collective-permute-start = (bf16[1,16,128]{2,1,0:T(8,128)(2,1)}, bf16[1,16,128]{2,1,0:T(8,128)(2,1)S(1)}, u32[]{:S(2)}, u32[]{:S(2)}) collective-permute-start(bf16[1,16,128]{2,1,0:T(8,128)(2,1)} %param.11), channel_id=1, source_target_pairs={{0,4},{1,2},{2,1},{3,7},{4,0},{5,6},{6,5},{7,3},{8,12},{9,10},{10,... | collective-permute-start | bytes 12296 | tf_op jit(solution)/shard_map/ppermute | solution.py:268
  1.2 6.0 %collective-permute-start.1 = (bf16[1,16,128]{2,1,0:T(8,128)(2,1)}, bf16[1,16,128]{2,1,0:T(8,128)(2,1)S(1)}, u32[]{:S(2)}, u32[]{:S(2)}) collective-permute-start(bf16[1,16,128]{2,1,0:T(8,128)(2,1)} %param.11), channel_id=1, source_target_pairs={{0,1},{1,0},{2,3},{3,2},{4,5},{5,4},{6,7},{7,6},{8,9},{9,8},{10,11... | collective-permute-start | bytes 12296 | tf_op jit(solution)/shard_map/ppermute | solution.py:268
  6.7 5.7 %copy-start = (bf16[3,64,192]{2,1,0:T(8,128)(2,1)S(1)}, bf16[3,64,192]{2,1,0:T(8,128)(2,1)}, u32[]{:S(2)}) copy-start(bf16[3,64,192]{2,1,0:T(8,128)(2,1)} %hidden_weights.1) | copy-start | bytes 221188
  7.4 1.2 %collective-permute-start.2 = (bf16[1,16,256]{2,1,0:T(8,128)(2,1)S(1)}, bf16[1,16,256]{2,1,0:T(8,128)(2,1)S(1)}, u32[]{:S(2)}, u32[]{:S(2)}) collective-permute-start(bf16[1,16,256]{2,1,0:T(8,128)(2,1)S(1)} %pad_maximum_fusion.1), channel_id=1, source_target_pairs={{0,4},{1,5},{2,6},{3,7},{4,0},{5,1},{6,2},{7,3},{8,12},{9,13},{10,... | collective-permute-start | bytes 24584 | tf_op jit(solution)/shard_map/ppermute | solution.py:268
  8.6 3.8 %copy-start.2 = (bf16[9,33]{1,0:T(8,128)(2,1)S(1)}, bf16[9,33]{1,0:T(8,128)(2,1)}, u32[]{:S(2)}) copy-start(bf16[9,33]{1,0:T(8,128)(2,1)} %designature.1) | copy-start | bytes 1786
  8.6 3.8 %copy-start.3 = (bf16[9,33]{1,0:T(8,128)(2,1)S(1)}, bf16[9,33]{1,0:T(8,128)(2,1)}, u32[]{:S(2)}) copy-start(bf16[9,33]{1,0:T(8,128)(2,1)} %shaping.1) | copy-start | bytes 1786
  8.6 3.8 %copy-start.7 = (bf16[64]{0:T(256)(128)(2,1)S(1)}, bf16[64]{0:T(256)(128)(2,1)}, u32[]{:S(2)}) copy-start(bf16[64]{0:T(256)(128)(2,1)} %param.19) | copy-start | bytes 388
  8.7 3.8 %copy-start.1 = (bf16[64,30]{0,1:T(8,128)(2,1)S(1)}, bf16[64,30]{0,1:T(8,128)(2,1)}, u32[]{:S(2)}) copy-start(bf16[64,30]{0,1:T(8,128)(2,1)} %param.15) | copy-start | bytes 11524
  8.7 4.9 %collective-permute-start.4 = (bf16[2,16,256]{2,1,0:T(8,128)(2,1)S(1)}, bf16[2,16,256]{2,1,0:T(8,128)(2,1)S(1)}, u32[]{:S(2)}, u32[]{:S(2)}) collective-permute-start(bf16[2,16,256]{2,1,0:T(8,128)(2,1)S(1)} %pad_maximum_fusion.pair), channel_id=1, source_target_pairs={{0,4},{1,5},{2,6},{3,7},{4,0},{5,1},{6,2},{7,3},{8,16},{9,17},{10,... | collective-permute-start | bytes 49160 | tf_op jit(solution)/shard_map/ppermute | solution.py:268
  8.9 4.7 %collective-permute-start.3 = (bf16[2,16,256]{2,1,0:T(8,128)(2,1)S(1)}, bf16[2,16,256]{2,1,0:T(8,128)(2,1)S(1)}, u32[]{:S(2)}, u32[]{:S(2)}) collective-permute-start(bf16[2,16,256]{2,1,0:T(8,128)(2,1)S(1)} %pad_maximum_fusion.pair), channel_id=1, source_target_pairs={{0,8},{1,9},{2,10},{3,11},{4,12},{5,13},{6,14},{7,15},{8,0},{9,1},... | collective-permute-start | bytes 49160 | tf_op jit(solution)/shard_map/ppermute | solution.py:268
  12.4 0.7 %copy-start.4 = (f32[3,64]{1,0:T(4,128)S(1)}, f32[3,64]{1,0:T(4,128)}, u32[]{:S(2)}) copy-start(f32[3,64]{1,0:T(4,128)} %hidden_bias.1) | copy-start | bytes 2308
  12.4 0.7 %copy-start.5 = (s32[8]{0:T(128)S(1)}, s32[8]{0:T(128)}, u32[]{:S(2)}) copy-start(s32[8]{0:T(128)} %param.13) | copy-start | bytes 100
  12.4 0.7 %copy-start.6 = (f32[64]{0:T(128)S(1)}, f32[64]{0:T(128)}, u32[]{:S(2)}) copy-start(f32[64]{0:T(128)} %param.16) | copy-start | bytes 772

commit v4 on v3

--- a/solution.py
+++ b/solution.py
@@ -7,11 +7,11 @@
 from jax.experimental.pallas import tpu as pltpu
 from jax.sharding import PartitionSpec as P
 
+
 HID = 3
 FN = 9
 FT = 33
 SHOT_TAPS = 5
-DMAX = 32
 LANES = 128
 VMEM_LIMIT = 24 * 2**20
 LEAD = 32
@@ -67,8 +67,8 @@
 
 
 def prepare(
-    dither, designature, shaping, first_weights, first_bias, hidden_weights, hidden_bias, out_weights, out_bias,
-    tt1, tt2, w0, wh, ow, small, pad
+    dither, designature, shaping, first_weights, first_bias, hidden_bias, out_weights, out_bias,
+    tt1, tt2, w0, wx, ow, small, pad
 ):
     window = tt1.shape[1]
     for taps, offset, out in ((designature, 0, tt1), (shaping, LEAD - FT // 2, tt2)):
@@ -93,17 +93,9 @@
     value = lax.dot_general(first_weights[...], select, (((0,), (0,)), ((), ())), preferred_element_type=F32)
     lanes = lax.broadcasted_iota(jnp.int32, w0.shape, 1)
     w0[...] = (value + extras(bias[:, 0:1], lanes, 48)).astype(BF16)
-    taps = hidden_weights.shape[2]
-    unit = jnp.where(
-        lax.broadcasted_iota(jnp.int32, (taps, wh.shape[2]), 0)
-        == lax.broadcasted_iota(jnp.int32, (taps, wh.shape[2]), 1),
-        1.0,
-        0.0,
-    ).astype(BF16)
-    lanes = lax.broadcasted_iota(jnp.int32, wh.shape[1:], 1)
+    lanes = lax.broadcasted_iota(jnp.int32, wx.shape[1:], 1)
     for layer in range(HID):
-        value = jnp.dot(hidden_weights[layer], unit, preferred_element_type=F32)
-        wh[layer] = (value + extras(bias[:, layer + 1 : layer + 2], lanes, taps)).astype(BF16)
+        wx[layer] = extras(bias[:, layer + 1 : layer + 2], lanes, 3 * channels).astype(BF16)
     nodes = ow.shape[0]
     row = out_weights[...].astype(F32)
     row = jnp.concatenate([row] * (LANES // channels), axis=1)
@@ -116,6 +108,25 @@
     small[1:2, :] = pad[0:1, 0:LANES]
 
 
+def frame_of(parts, even, odd, mine, out):
+    t = lax.axis_index("tm")
+    samples, span = mine.shape[2], out.shape[2]
+    x = mine[0].astype(F32)
+    alive = x[:, 0:1] < LIMIT
+    a, b = even[0].astype(F32), odd[0].astype(F32)
+    is_even = t % 2 == 0
+    left = jnp.where(t == 0, 0.0, jnp.where(is_even, b, a))
+    right = jnp.where(t == parts - 1, 0.0, jnp.where(is_even, a, b))
+    left, right = jnp.where(alive, left, DEAD), jnp.where(alive, right, DEAD)
+    gap = jnp.zeros((x.shape[0], span - samples), F32)
+    lanes = lax.broadcasted_iota(jnp.int32, (x.shape[0], span), 1)
+    spread = [jnp.concatenate([v, gap], axis=1) for v in (left, x, right)]
+    left = pltpu.roll(spread[0], span + BEFORE - samples, 1)
+    x, right = pltpu.roll(spread[1], BEFORE, 1), pltpu.roll(spread[2], (BEFORE + samples) % span, 1)
+    x = jnp.where(lanes < BEFORE, left, jnp.where(lanes < BEFORE + samples, x, right))
+    out[0] = x.astype(BF16)
+
+
 def moved(tiles, by):
     n = len(tiles)
     lanes = lax.broadcasted_iota(jnp.int32, tiles[0].shape, 1)
@@ -139,7 +150,8 @@
     tt1,
     tt2,
     w0,
-    wh,
+    hidden,
+    wx,
     ow,
     small,
     interference,
@@ -147,26 +159,30 @@
     xn,
     gs,
     zp,
+    wh,
 ):
     nodes, samples = interference.shape
     windows = samples // LANES + 1
     span = windows * LANES
     window = 2 * LANES
-    channels = w0.shape[0]
     rows = nodes * 8
     t, s = lax.axis_index("tm"), lax.axis_index("shot")
     chip = s // 2
     even = chip % 2 == 0
     lowest, highest = chip == 0, chip == shots // 2 - 1
     zero = jnp.zeros((nodes, LANES), F32)
-    own_live = []
+    depth = hidden.shape[2]
+    wh[...] = wx[...]
+    wh[:, :, 0:depth] = hidden[...]
+    odd = s % 2 == 1
+    alive = pair[0].astype(F32)[:, BEFORE : BEFORE + 1] < LIMIT
+    near = [[jnp.where(odd, v[1 - j].astype(F32), v[j].astype(F32)) for j in range(2)] for v in (pair, first, second)]
     for j in range(8):
         if 2 <= j < 4:
-            x = pair[j - 2].astype(F32)
-            own_live.append(x[:, BEFORE : BEFORE + 1])
+            x = near[0][j - 2]
         elif j < 6:
-            p, q = (second, first) if j < 2 else (first, second)
-            x = jnp.where(even, p[j % 2].astype(F32), q[j % 2].astype(F32))
+            p, q = (2, 1) if j < 2 else (1, 2)
+            x = jnp.where(even, near[p][j % 2], near[q][j % 2])
             x = jnp.where(lowest if j < 2 else highest, 0.0, x)
         for w in range(windows):
             xn[pl.ds(w * rows + j, nodes, stride=8), :] = zero if j >= 6 else x[:, w * LANES : (w + 1) * LANES]
@@ -220,13 +236,11 @@
         for n in range(nodes):
             tiles = [acts[n][:, w * LANES : (w + 1) * LANES] for w in range(windows)]
             columns = jnp.concatenate(taps_of(tiles, 2 ** (layer + 1)) + [extra], axis=0)
-            act = jnp.dot(wh[layer], columns, preferred_element_type=F32)
+            act = jnp.dot(wh[layer][:, 0 : depth + 16], columns, preferred_element_type=F32)
             acts[n] = jnp.maximum(act.astype(BF16), 0.0)
     pred = jnp.dot(ow[...], jnp.concatenate(acts, axis=0), preferred_element_type=F32) + small[0:1, 0:1]
     pred = pred.astype(BF16).astype(F32)
-    odd = s % 2 == 1
     own = jnp.where(odd, own[1], own[0])
-    alive = jnp.where(odd, own_live[1], own_live[0]) < LIMIT
     pred = jnp.where(alive & valid, pred, 0.0)
     interference[...] = pltpu.roll(pred, span - LEAD, 1)[:, 0:samples].astype(BF16)
     difference = (own - pred).astype(BF16)
@@ -262,27 +276,28 @@
     window = 2 * LANES
     windows = samples // LANES + 1
     span = windows * LANES
-    frame = span
-    s, t = lax.axis_index("shot"), lax.axis_index("tm")
     time_even, time_odd, partner, pair_even, pair_odd = exchanges(shots, parts)
-    send = lambda x, pairs: lax.ppermute(x, AXES, pairs)
+
+    def send(x, pairs):
+        return lax.ppermute(x, AXES, pairs)
+
 
     vmem = pl.BlockSpec(memory_space=pltpu.VMEM)
-    tt1, tt2, w0, wh, ow, small = pl.pallas_call(
+    tt1, tt2, w0, wx, ow, small = pl.pallas_call(
         prepare,
         out_shape=(
             jax.ShapeDtypeStruct((FN * LANES, window), BF16),
             jax.ShapeDtypeStruct((FN * LANES, window), BF16),
             jax.ShapeDtypeStruct((channels, 64), BF16),
-            jax.ShapeDtypeStruct((HID, channels, 3 * channels + 16), BF16),
+            jax.ShapeDtypeStruct((HID, channels, window), BF16),
             jax.ShapeDtypeStruct((nodes, nodes * channels), BF16),
             jax.ShapeDtypeStruct((8, LANES), F32),
         ),
-        in_specs=[vmem] * 9,
+        in_specs=[vmem] * 8,
         out_specs=(vmem,) * 6,
         scratch_shapes=[pltpu.VMEM((16, window), F32)],
         compiler_params=pltpu.CompilerParams(vmem_limit_bytes=VMEM_LIMIT),
-        cost_estimate=pl.CostEstimate(flops=4 * 10**6, bytes_accessed=10**6, transcendentals=0),
+        cost_estimate=pl.CostEstimate(flops=10**8, bytes_accessed=10**7, transcendentals=0),
         name="prepare",
     )(
         dither[None],
@@ -290,7 +305,6 @@
         shaping,
         first_weights.T,
         first_bias[None],
-        hidden_weights,
         hidden_bias,
         out_weights[None],
         out_bias[None],
@@ -300,31 +314,32 @@
     dead = jnp.asarray(DEAD, BF16)
     a, b = send(records, time_even), send(records, time_odd)
     mine = lax.optimization_barrier(jnp.where(keep, records, dead))
-    t_even = t % 2 == 0
-    left = jnp.where(t_even, b, a)[:, :, samples - BEFORE :]
-    right = jnp.where(t_even, a, b)[:, :, : frame - BEFORE - samples]
-    left = jnp.where(t == 0, jnp.zeros_like(left), left)
-    right = jnp.where(t == parts - 1, jnp.zeros_like(right), right)
-    x = jnp.concatenate([jnp.where(keep, left, dead), mine, jnp.where(keep, right, dead)], axis=2)
-    y = send(x, partner)
-    s_even = s % 2 == 0
-    pair = jnp.concatenate([jnp.where(s_even, x, y), jnp.where(s_even, y, x)], axis=0)
+    x = pl.pallas_call(
+        functools.partial(frame_of, parts),
+        out_shape=jax.ShapeDtypeStruct((1, nodes, span), BF16),
+        in_specs=[vmem] * 3,
+        out_specs=vmem,
+        compiler_params=pltpu.CompilerParams(vmem_limit_bytes=VMEM_LIMIT),
+        name="frame",
+    )(a, b, mine)
+    pair = jnp.concatenate([x, send(x, partner)], axis=0)
     first, second = send(pair, pair_even), send(pair, pair_odd)
 
     interference, cleaned = pl.pallas_call(
         functools.partial(deblend, total, shots),
         out_shape=(jax.ShapeDtypeStruct((nodes, samples), BF16),) * 2,
-        in_specs=[vmem] * 9,
+        in_specs=[vmem] * 10,
         out_specs=(vmem,) * 2,
         scratch_shapes=[
             pltpu.VMEM((windows * nodes * 8, LANES), F32),
             pltpu.VMEM((windows * nodes * 16, LANES), F32),
             pltpu.VMEM((nodes + 16, FN * LANES), F32),
+            pltpu.VMEM((HID, channels, window), BF16),
         ],
         compiler_params=pltpu.CompilerParams(vmem_limit_bytes=VMEM_LIMIT),
         cost_estimate=pl.CostEstimate(flops=4 * 10**8, bytes_accessed=10**6, transcendentals=0),
         name="deblend",
-    )(pair, first, second, tt1, tt2, w0, wh, ow, small)
+    )(pair, first, second, tt1, tt2, w0, hidden_weights, wx, ow, small)
     return interference[None], cleaned[None]
 
 
@@ -332,5 +347,8 @@
     shots, parts = mesh.shape["shot"], mesh.shape["tm"]
     in_specs = (P("shot", None, "tm"), P("shot", None), P(), P(), P(), P(), P(), P(), P(), P(), P())
     out_specs = (P("shot", None, "tm"), P("shot", None, "tm"))
-    body = functools.partial(local, shots=shots, parts=parts)
+
+    def body(*args):
+        return local(*args, shots=shots, parts=parts)
+
     return jax.shard_map(body, mesh=mesh, in_specs=in_specs, out_specs=out_specs, check_vma=False)

time: 16.7 us -> 15.9 us (0.952)
  the two profiles are of different devices: /device:TPU:0 before, /device:TPU:18 now
where the time goes in v4:
time: 15.9 us; the launch traced here: 15.6 us
  waiting for transfers between devices  5.46 us (34%)
  Pallas kernels  3.51 us (22%)
  starting transfers between devices  3.21 us (20%)
  other arithmetic  1.42 us (9%)
  between operations  1.37 us (9%)
  local copies, waits for them, and re-layouts  0.65 us (4%)
    ppermute x5, waiting for transfers between devices, send(): return lax.ppermute(x, AXES, pairs)  5.46 us
    ppermute x5, starting transfers between devices, send(): return lax.ppermute(x, AXES, pairs)  3.21 us
    pallas_call x1, Pallas kernels, local(): pl.pallas_call(functools.partial(deblend, total, shots), out_shape=(jax.S...  2.89 us
    select_n x1, other arithmetic, local(): mine = lax.optimization_barrier(jnp.where(keep, records, dead))  0.76 us
    gt x1, other arithmetic, local(): keep = live[:, :, None] > 0  0.66 us
    unnamed x16, local copies, waits for them, and re-layouts  0.65 us
    pallas_call x1, Pallas kernels, local(): pl.pallas_call(prepare, out_shape=(jax.ShapeDtypeStruct((FN * LANES, wind...  0.48 us
  transfers between devices with their start and end apart: 5, of which 5 were waited for; matrix products, arithmetic and copies ran while one was open for 9% of the time, Pallas kernels for 3%

profile of v4, /device:TPU:18, one launch (start us, length us, event | category | flops | bytes accessed | tf_op | source)
XLA Modules:
  0.0 15.6 jit_solution(3990598093933018144)
XLA Ops:
  0.6 1.6 %collective-permute-start = (bf16[1,16,128]{2,1,0:T(8,128)(2,1)}, bf16[1,16,128]{2,1,0:T(8,128)(2,1)S(1)}, u32[]{:S(2)}, u32[]{:S(2)}) collective-permute-start(bf16[1,16,128]{2,1,0:T(8,128)(2,1)} %param.11), channel_id=1, source_target_pairs={{0,1},{1,0},{2,3},{3,2},{4,5},{5,4},{6,7},{7,6},{8,9},{9,8},{10,11... | collective-permute-start | bytes 12296 | tf_op jit(solution)/shard_map/ppermute | solution.py:282
  2.3 0.0 collective-permute-start.1
  2.3 0.7 %compare_bitcast_fusion = pred[16]{0:T(512)(128)(4,1)S(1)} fusion(s32[1,16]{1,0:T(1,128)} %param.12), kind=kLoop, calls=%fused_computation.2 | loop fusion | flops 16 | bytes 80 | tf_op jit(solution)/shard_map/gt | solution.py:313
  2.9 0.8 %broadcast_select_fusion.mine = bf16[1,16,128]{2,1,0:T(8,128)(2,1)S(1)} fusion(bf16[1,16,128]{2,1,0:T(8,128)(2,1)} %param.11, pred[16]{0:T(512)(128)(4,1)S(1)} %compare_bitcast_fusion), kind=kLoop, calls=%fused_computation.1 | loop fusion | flops 2048 | bytes 8208 | tf_op jit(solution)/shard_map/jit(_where)/select_n | solution.py:316
  3.7 0.8 %collective-permute-done.even = bf16[1,16,128]{2,1,0:T(8,128)(2,1)S(1)} collective-permute-done((bf16[1,16,128]{2,1,0:T(8,128)(2,1)}, bf16[1,16,128]{2,1,0:T(8,128)(2,1)S(1)}, u32[]{:S(2)}, u32[]{:S(2)}) %collective-permute-start) | collective-permute-done | bytes 4128 | tf_op jit(solution)/shard_map/ppermute | solution.py:282
  4.5 1.6 %collective-permute-done.1.odd = bf16[1,16,128]{2,1,0:T(8,128)(2,1)S(1)} collective-permute-done((bf16[1,16,128]{2,1,0:T(8,128)(2,1)}, bf16[1,16,128]{2,1,0:T(8,128)(2,1)S(1)}, u32[]{:S(2)}, u32[]{:S(2)}) %collective-permute-start.1) | collective-permute-done | bytes 4128 | tf_op jit(solution)/shard_map/ppermute | solution.py:282
  6.1 0.1 frame.1
  6.2 0.0 collective-permute-start.2
  6.3 1.2 %collective-permute-done.2 = bf16[1,16,256]{2,1,0:T(8,128)(2,1)S(1)} collective-permute-done((bf16[1,16,256]{2,1,0:T(8,128)(2,1)S(1)}, bf16[1,16,256]{2,1,0:T(8,128)(2,1)S(1)}, u32[]{:S(2)}, u32[]{:S(2)}) %collective-permute-start.2) | collective-permute-done | bytes 8224 | tf_op jit(solution)/shard_map/ppermute | solution.py:282
  7.4 0.0 copy-start.1
  7.4 1.6 %collective-permute-start.4 = (bf16[2,16,256]{2,1,0:T(8,128)(2,1)S(1)}, bf16[2,16,256]{2,1,0:T(8,128)(2,1)S(1)}, u32[]{:S(2)}, u32[]{:S(2)}) collective-permute-start(bf16[2,16,256]{2,1,0:T(8,128)(2,1)S(1)} %pad_maximum_fusion.pair), channel_id=1, source_target_pairs={{0,4},{1,5},{2,6},{3,7},{4,0},{5,1},{6,2},{7,3},{8,16},{9,17},{10,... | collective-permute-start | bytes 49160 | tf_op jit(solution)/shard_map/ppermute | solution.py:282
  9.0 0.0 collective-permute-start.3
  9.7 0.0 copy-start.4
  9.7 0.0 copy-start.5
  9.7 0.0 copy-start.6
  9.7 0.0 copy-done.2
  9.7 0.0 copy-done.3
  9.7 0.0 copy-done.7
  9.7 0.6 %copy-done.4 = f32[3,64]{1,0:T(4,128)S(1)} copy-done((f32[3,64]{1,0:T(4,128)S(1)}, f32[3,64]{1,0:T(4,128)}, u32[]{:S(2)}) %copy-start.4) | copy-done | bytes 792
  10.3 0.0 copy-done.5
  10.3 0.5 %prepare.1 = (bf16[1152,256]{1,0:T(8,128)(2,1)S(1)}, bf16[1152,256]{1,0:T(8,128)(2,1)S(1)}, bf16[64,64]{1,0:T(8,128)(2,1)S(1)}, bf16[3,64,256]{2,1,0:T(8,128)(2,...) custom-call(s32[1,8]{1,0:T(1,128)S(1)} %bitcast.11, bf16[9,33]{1,0:T(8,128)(2,1)S(1)} %copy-done.2, ...), custom_call_target="tpu_custom_call" | custom-call | flops 100000000 | bytes 10000000 | tf_op jit(solution)/shard_map/prepare/pallas_call | solution.py:286
  10.8 1.3 %collective-permute-done.4.second = bf16[2,16,256]{2,1,0:T(8,128)(2,1)S(1)} collective-permute-done((bf16[2,16,256]{2,1,0:T(8,128)(2,1)S(1)}, bf16[2,16,256]{2,1,0:T(8,128)(2,1)S(1)}, u32[]{:S(2)}, u32[]{:S(2)}) %collective-permute-start.4) | collective-permute-done | bytes 16416 | tf_op jit(solution)/shard_map/ppermute | solution.py:282
  12.1 0.6 %collective-permute-done.3.first = bf16[2,16,256]{2,1,0:T(8,128)(2,1)S(1)} collective-permute-done((bf16[2,16,256]{2,1,0:T(8,128)(2,1)S(1)}, bf16[2,16,256]{2,1,0:T(8,128)(2,1)S(1)}, u32[]{:S(2)}, u32[]{:S(2)}) %collective-permute-start.3) | collective-permute-done | bytes 16416 | tf_op jit(solution)/shard_map/ppermute | solution.py:282
  12.7 2.9 %deblend.1 = (bf16[16,128]{1,0:T(8,128)(2,1)}, bf16[16,128]{1,0:T(8,128)(2,1)}) custom-call(bf16[2,16,256]{2,1,0:T(8,128)(2,1)S(1)} %pad_maximum_fusion.pair, bf16[2,16,256]{2,1,0:T(8,128)(2,1)S(1)} %collective-permute-done.3.first, bf16[2,16,256]{2,1,0:T(8,128)(2,1)S(1)} %collective-permute-done.4.second, bf16[1152,256]{1,0:T(8,128)(2,1)S(1)} %get-tuple-element.10.tt1, ...), custom_call_target="tpu_custom_call" | custom-call | flops 400000000 | bytes 1000000 | tf_op jit(solution)/shard_map/deblend/pallas_call | solution.py:328
  (8 shorter events, 0.0 us)
Async XLA Ops:
  0.6 3.9 %collective-permute-start = (bf16[1,16,128]{2,1,0:T(8,128)(2,1)}, bf16[1,16,128]{2,1,0:T(8,128)(2,1)S(1)}, u32[]{:S(2)}, u32[]{:S(2)}) collective-permute-start(bf16[1,16,128]{2,1,0:T(8,128)(2,1)} %param.11), channel_id=1, source_target_pairs={{0,1},{1,0},{2,3},{3,2},{4,5},{5,4},{6,7},{7,6},{8,9},{9,8},{10,11... | collective-permute-start | bytes 12296 | tf_op jit(solution)/shard_map/ppermute | solution.py:282
  2.3 3.8 %collective-permute-start.1 = (bf16[1,16,128]{2,1,0:T(8,128)(2,1)}, bf16[1,16,128]{2,1,0:T(8,128)(2,1)S(1)}, u32[]{:S(2)}, u32[]{:S(2)}) collective-permute-start(bf16[1,16,128]{2,1,0:T(8,128)(2,1)} %param.11), channel_id=1, source_target_pairs={{0,4},{1,2},{2,1},{3,7},{4,0},{5,6},{6,5},{7,3},{8,12},{9,10},{10,... | collective-permute-start | bytes 12296 | tf_op jit(solution)/shard_map/ppermute | solution.py:282
  6.2 1.2 %collective-permute-start.2 = (bf16[1,16,256]{2,1,0:T(8,128)(2,1)S(1)}, bf16[1,16,256]{2,1,0:T(8,128)(2,1)S(1)}, u32[]{:S(2)}, u32[]{:S(2)}) collective-permute-start(bf16[1,16,256]{2,1,0:T(8,128)(2,1)S(1)} %frame.1), channel_id=1, source_target_pairs={{0,4},{1,5},{2,6},{3,7},{4,0},{5,1},{6,2},{7,3},{8,12},{9,13},{10,... | collective-permute-start | bytes 24584 | tf_op jit(solution)/shard_map/ppermute | solution.py:282
  7.4 2.3 %copy-start.2 = (bf16[9,33]{1,0:T(8,128)(2,1)S(1)}, bf16[9,33]{1,0:T(8,128)(2,1)}, u32[]{:S(2)}) copy-start(bf16[9,33]{1,0:T(8,128)(2,1)} %designature.1) | copy-start | bytes 1786
  7.4 2.3 %copy-start.3 = (bf16[9,33]{1,0:T(8,128)(2,1)S(1)}, bf16[9,33]{1,0:T(8,128)(2,1)}, u32[]{:S(2)}) copy-start(bf16[9,33]{1,0:T(8,128)(2,1)} %shaping.1) | copy-start | bytes 1786
  7.4 2.3 %copy-start.7 = (bf16[64]{0:T(256)(128)(2,1)S(1)}, bf16[64]{0:T(256)(128)(2,1)}, u32[]{:S(2)}) copy-start(bf16[64]{0:T(256)(128)(2,1)} %param.19) | copy-start | bytes 388
  7.4 2.3 %copy-start.1 = (bf16[64,30]{0,1:T(8,128)(2,1)S(1)}, bf16[64,30]{0,1:T(8,128)(2,1)}, u32[]{:S(2)}) copy-start(bf16[64,30]{0,1:T(8,128)(2,1)} %param.15) | copy-start | bytes 11524
  7.4 4.7 %collective-permute-start.4 = (bf16[2,16,256]{2,1,0:T(8,128)(2,1)S(1)}, bf16[2,16,256]{2,1,0:T(8,128)(2,1)S(1)}, u32[]{:S(2)}, u32[]{:S(2)}) collective-permute-start(bf16[2,16,256]{2,1,0:T(8,128)(2,1)S(1)} %pad_maximum_fusion.pair), channel_id=1, source_target_pairs={{0,4},{1,5},{2,6},{3,7},{4,0},{5,1},{6,2},{7,3},{8,16},{9,17},{10,... | collective-permute-start | bytes 49160 | tf_op jit(solution)/shard_map/ppermute | solution.py:282
  9.0 3.7 %collective-permute-start.3 = (bf16[2,16,256]{2,1,0:T(8,128)(2,1)S(1)}, bf16[2,16,256]{2,1,0:T(8,128)(2,1)S(1)}, u32[]{:S(2)}, u32[]{:S(2)}) collective-permute-start(bf16[2,16,256]{2,1,0:T(8,128)(2,1)S(1)} %pad_maximum_fusion.pair), channel_id=1, source_target_pairs={{0,8},{1,9},{2,10},{3,11},{4,12},{5,13},{6,14},{7,15},{8,0},{9,1},... | collective-permute-start | bytes 49160 | tf_op jit(solution)/shard_map/ppermute | solution.py:282
  9.7 0.7 %copy-start.4 = (f32[3,64]{1,0:T(4,128)S(1)}, f32[3,64]{1,0:T(4,128)}, u32[]{:S(2)}) copy-start(f32[3,64]{1,0:T(4,128)} %hidden_bias.1) | copy-start | bytes 2308
  9.7 0.7 %copy-start.5 = (s32[8]{0:T(128)S(1)}, s32[8]{0:T(128)}, u32[]{:S(2)}) copy-start(s32[8]{0:T(128)} %param.13) | copy-start | bytes 100
  9.7 0.7 %copy-start.6 = (f32[64]{0:T(128)S(1)}, f32[64]{0:T(128)}, u32[]{:S(2)}) copy-start(f32[64]{0:T(128)} %param.16) | copy-start | bytes 772
  10.3 2.4 %copy-start = (bf16[3,64,192]{2,1,0:T(8,128)(2,1)S(1)}, bf16[3,64,192]{2,1,0:T(8,128)(2,1)}, u32[]{:S(2)}) copy-start(bf16[3,64,192]{2,1,0:T(8,128)(2,1)} %hidden.1) | copy-start | bytes 221188

commit v5 on v4

--- a/solution.py
+++ b/solution.py
@@ -34,22 +34,26 @@
 
 
 def exchanges(shots, parts):
-    def time_odd(s, t):
-        o = ((t + 1) ^ 1) - 1
-        return (s, o) if 0 <= o < parts else (s ^ 1, t)
-
-    def pair_odd(s, t):
-        o = ((s // 2 + 1) ^ 1) - 1
-        return (2 * o + s % 2, t) if 0 <= o < shots // 2 else (s ^ 1, t)
-
-    rules = (
-        lambda s, t: (s, t ^ 1),
-        time_odd,
-        lambda s, t: (s ^ 1, t),
-        lambda s, t: (s ^ 2, t),
-        pair_odd,
-    )
-    return [partners(shots, parts, rule) for rule in rules]
+    def meet(i, n, k):
+        if i % 3 == k and i + 1 < n:
+            return i + 1
+        return i - 1 if i % 3 == (k + 1) % 3 and i > 0 else i
+
+    def along_time(s, t, k):
+        o = meet(t, parts, k)
+        return (s ^ 1, t) if o == t else (s, o)
+
+    def along_shot(s, t, k):
+        o = meet(s // 2, shots // 2, k)
+        return (s ^ 1, t) if o == s // 2 else (2 * o + s % 2, t)
+
+    times = [partners(shots, parts, functools.partial(along_time, k=k)) for k in range(3)]
+    pairs = [partners(shots, parts, functools.partial(along_shot, k=k)) for k in range(3)]
+    return times, partners(shots, parts, lambda s, t: (s ^ 1, t)), pairs
+
+
+def pick(index, values):
+    return jnp.where(index == 0, values[0], jnp.where(index == 1, values[1], values[2]))
 
 
 def contract_lanes(a, b):
@@ -108,15 +112,14 @@
     small[1:2, :] = pad[0:1, 0:LANES]
 
 
-def frame_of(parts, even, odd, mine, out):
+def frame_of(parts, first, second, third, mine, out):
     t = lax.axis_index("tm")
     samples, span = mine.shape[2], out.shape[2]
     x = mine[0].astype(F32)
     alive = x[:, 0:1] < LIMIT
-    a, b = even[0].astype(F32), odd[0].astype(F32)
-    is_even = t % 2 == 0
-    left = jnp.where(t == 0, 0.0, jnp.where(is_even, b, a))
-    right = jnp.where(t == parts - 1, 0.0, jnp.where(is_even, a, b))
+    got = [v[0].astype(F32) for v in (first, second, third)]
+    left = jnp.where(t == 0, 0.0, pick((t + 2) % 3, got))
+    right = jnp.where(t == parts - 1, 0.0, pick(t % 3, got))
     left, right = jnp.where(alive, left, DEAD), jnp.where(alive, right, DEAD)
     gap = jnp.zeros((x.shape[0], span - samples), F32)
     lanes = lax.broadcasted_iota(jnp.int32, (x.shape[0], span), 1)
@@ -147,6 +150,7 @@
     pair,
     first,
     second,
+    third,
     tt1,
     tt2,
     w0,
@@ -168,7 +172,6 @@
     rows = nodes * 8
     t, s = lax.axis_index("tm"), lax.axis_index("shot")
     chip = s // 2
-    even = chip % 2 == 0
     lowest, highest = chip == 0, chip == shots // 2 - 1
     zero = jnp.zeros((nodes, LANES), F32)
     depth = hidden.shape[2]
@@ -176,13 +179,13 @@
     wh[:, :, 0:depth] = hidden[...]
     odd = s % 2 == 1
     alive = pair[0].astype(F32)[:, BEFORE : BEFORE + 1] < LIMIT
-    near = [[jnp.where(odd, v[1 - j].astype(F32), v[j].astype(F32)) for j in range(2)] for v in (pair, first, second)]
+    near = [[jnp.where(odd, v[1 - j].astype(F32), v[j].astype(F32)) for j in range(2)] for v in (pair, first, second, third)]
     for j in range(8):
         if 2 <= j < 4:
             x = near[0][j - 2]
         elif j < 6:
-            p, q = (2, 1) if j < 2 else (1, 2)
-            x = jnp.where(even, near[p][j % 2], near[q][j % 2])
+            turn = (chip + 2) % 3 if j < 2 else chip % 3
+            x = pick(turn, [v[j % 2] for v in near[1:]])
             x = jnp.where(lowest if j < 2 else highest, 0.0, x)
         for w in range(windows):
             xn[pl.ds(w * rows + j, nodes, stride=8), :] = zero if j >= 6 else x[:, w * LANES : (w + 1) * LANES]
@@ -276,7 +279,7 @@
     window = 2 * LANES
     windows = samples // LANES + 1
     span = windows * LANES
-    time_even, time_odd, partner, pair_even, pair_odd = exchanges(shots, parts)
+    times, partner, pairs = exchanges(shots, parts)
 
     def send(x, pairs):
         return lax.ppermute(x, AXES, pairs)
@@ -312,23 +315,23 @@
 
     keep = live[:, :, None] > 0
     dead = jnp.asarray(DEAD, BF16)
-    a, b = send(records, time_even), send(records, time_odd)
+    around = [send(records, times[k]) for k in range(3)]
     mine = lax.optimization_barrier(jnp.where(keep, records, dead))
     x = pl.pallas_call(
         functools.partial(frame_of, parts),
         out_shape=jax.ShapeDtypeStruct((1, nodes, span), BF16),
-        in_specs=[vmem] * 3,
+        in_specs=[vmem] * 4,
         out_specs=vmem,
         compiler_params=pltpu.CompilerParams(vmem_limit_bytes=VMEM_LIMIT),
         name="frame",
-    )(a, b, mine)
+    )(*around, mine)
     pair = jnp.concatenate([x, send(x, partner)], axis=0)
-    first, second = send(pair, pair_even), send(pair, pair_odd)
+    near = [send(pair, pairs[k]) for k in range(3)]
 
     interference, cleaned = pl.pallas_call(
         functools.partial(deblend, total, shots),
         out_shape=(jax.ShapeDtypeStruct((nodes, samples), BF16),) * 2,
-        in_specs=[vmem] * 10,
+        in_specs=[vmem] * 11,
         out_specs=(vmem,) * 2,
         scratch_shapes=[
             pltpu.VMEM((windows * nodes * 8, LANES), F32),
@@ -339,7 +342,7 @@
         compiler_params=pltpu.CompilerParams(vmem_limit_bytes=VMEM_LIMIT),
         cost_estimate=pl.CostEstimate(flops=4 * 10**8, bytes_accessed=10**6, transcendentals=0),
         name="deblend",
-    )(pair, first, second, tt1, tt2, w0, hidden_weights, wx, ow, small)
+    )(pair, *near, tt1, tt2, w0, hidden_weights, wx, ow, small)
     return interference[None], cleaned[None]
 
 

time: 15.9 us -> 18.3 us (1.15)
  the two profiles are of different devices: /device:TPU:18 before, /device:TPU:0 now
where the time goes in v5:
time: 18.3 us; the launch traced here: 18.1 us
  starting transfers between devices  9.36 us (51%)
  Pallas kernels  3.47 us (19%)
  waiting for transfers between devices  1.5 us (8%)
  other arithmetic  1.42 us (8%)
  between operations  1.38 us (8%)
  local copies, waits for them, and re-layouts  0.99 us (5%)
    ppermute x7, starting transfers between devices, send(): return lax.ppermute(x, AXES, pairs)  9.36 us
    pallas_call x1, Pallas kernels, local(): pl.pallas_call(functools.partial(deblend, total, shots), out_shape=(jax.S...  2.85 us
    ppermute x7, waiting for transfers between devices, send(): return lax.ppermute(x, AXES, pairs)  1.5 us
    unnamed x16, local copies, waits for them, and re-layouts  0.99 us
    select_n x1, other arithmetic, local(): mine = lax.optimization_barrier(jnp.where(keep, records, dead))  0.76 us
    gt x1, other arithmetic, local(): keep = live[:, :, None] > 0  0.66 us
    pallas_call x1, Pallas kernels, local(): pl.pallas_call(prepare, out_shape=(jax.ShapeDtypeStruct((FN * LANES, wind...  0.48 us
  transfers between devices with their start and end apart: 7, of which 2 were waited for; matrix products, arithmetic and copies ran while one was open for 8% of the time, Pallas kernels for 3%

profile of v5, /device:TPU:0, one launch (start us, length us, event | category | flops | bytes accessed | tf_op | source)
XLA Modules:
  0.0 18.1 jit_solution(10256036089244089876)
XLA Ops:
  0.6 0.6 %collective-permute-start.1 = (bf16[1,16,128]{2,1,0:T(8,128)(2,1)}, bf16[1,16,128]{2,1,0:T(8,128)(2,1)S(1)}, u32[]{:S(2)}, u32[]{:S(2)}) collective-permute-start(bf16[1,16,128]{2,1,0:T(8,128)(2,1)} %param.11), channel_id=1, source_target_pairs={{0,4},{1,2},{2,1},{3,7},{4,0},{5,6},{6,5},{7,3},{8,12},{9,10},{10,... | collective-permute-start | bytes 12296 | tf_op jit(solution)/shard_map/ppermute | solution.py:285
  1.2 4.1 %collective-permute-start = (bf16[1,16,128]{2,1,0:T(8,128)(2,1)}, bf16[1,16,128]{2,1,0:T(8,128)(2,1)S(1)}, u32[]{:S(2)}, u32[]{:S(2)}) collective-permute-start(bf16[1,16,128]{2,1,0:T(8,128)(2,1)} %param.11), channel_id=1, source_target_pairs={{0,1},{1,0},{2,6},{3,7},{4,5},{5,4},{6,2},{7,3},{8,9},{9,8},{10,14... | collective-permute-start | bytes 12296 | tf_op jit(solution)/shard_map/ppermute | solution.py:285
  5.3 0.0 collective-permute-start.2
  5.3 0.7 %compare_bitcast_fusion = pred[16]{0:T(512)(128)(4,1)S(1)} fusion(s32[1,16]{1,0:T(1,128)} %param.12), kind=kLoop, calls=%fused_computation.2 | loop fusion | flops 16 | bytes 80 | tf_op jit(solution)/shard_map/gt | solution.py:316
  6.0 0.8 %broadcast_select_fusion.mine = bf16[1,16,128]{2,1,0:T(8,128)(2,1)S(1)} fusion(bf16[1,16,128]{2,1,0:T(8,128)(2,1)} %param.11, pred[16]{0:T(512)(128)(4,1)S(1)} %compare_bitcast_fusion), kind=kLoop, calls=%fused_computation.1 | loop fusion | flops 2048 | bytes 8208 | tf_op jit(solution)/shard_map/jit(_where)/select_n | solution.py:319
  6.7 0.0 collective-permute-done.1.second
  6.8 0.4 %collective-permute-done.first = bf16[1,16,128]{2,1,0:T(8,128)(2,1)S(1)} collective-permute-done((bf16[1,16,128]{2,1,0:T(8,128)(2,1)}, bf16[1,16,128]{2,1,0:T(8,128)(2,1)S(1)}, u32[]{:S(2)}, u32[]{:S(2)}) %collective-permute-start) | collective-permute-done | bytes 4128 | tf_op jit(solution)/shard_map/ppermute | solution.py:285
  7.2 0.1 frame.1
  7.3 0.1 collective-permute-start.3
  7.4 1.1 %collective-permute-done.3 = bf16[1,16,256]{2,1,0:T(8,128)(2,1)S(1)} collective-permute-done((bf16[1,16,256]{2,1,0:T(8,128)(2,1)S(1)}, bf16[1,16,256]{2,1,0:T(8,128)(2,1)S(1)}, u32[]{:S(2)}, u32[]{:S(2)}) %collective-permute-start.3) | collective-permute-done | bytes 8224 | tf_op jit(solution)/shard_map/ppermute | solution.py:285
  8.5 0.0 copy-start.1
  8.5 0.2 %collective-permute-start.6 = (bf16[2,16,256]{2,1,0:T(8,128)(2,1)S(1)}, bf16[2,16,256]{2,1,0:T(8,128)(2,1)S(1)}, u32[]{:S(2)}, u32[]{:S(2)}) collective-permute-start(bf16[2,16,256]{2,1,0:T(8,128)(2,1)S(1)} %pad_maximum_fusion.pair), channel_id=1, source_target_pairs={{0,4},{1,5},{2,6},{3,7},{4,0},{5,1},{6,2},{7,3},{8,12},{9,13},{10,... | collective-permute-start | bytes 49160 | tf_op jit(solution)/shard_map/ppermute | solution.py:285
  8.7 0.3 %collective-permute-start.5 = (bf16[2,16,256]{2,1,0:T(8,128)(2,1)S(1)}, bf16[2,16,256]{2,1,0:T(8,128)(2,1)S(1)}, u32[]{:S(2)}, u32[]{:S(2)}) collective-permute-start(bf16[2,16,256]{2,1,0:T(8,128)(2,1)S(1)} %pad_maximum_fusion.pair), channel_id=1, source_target_pairs={{0,4},{1,5},{2,6},{3,7},{4,0},{5,1},{6,2},{7,3},{8,16},{9,17},{10,... | collective-permute-start | bytes 49160 | tf_op jit(solution)/shard_map/ppermute | solution.py:285
  9.1 4.0 %collective-permute-start.4 = (bf16[2,16,256]{2,1,0:T(8,128)(2,1)S(1)}, bf16[2,16,256]{2,1,0:T(8,128)(2,1)S(1)}, u32[]{:S(2)}, u32[]{:S(2)}) collective-permute-start(bf16[2,16,256]{2,1,0:T(8,128)(2,1)S(1)} %pad_maximum_fusion.pair), channel_id=1, source_target_pairs={{0,8},{1,9},{2,10},{3,11},{4,12},{5,13},{6,14},{7,15},{8,0},{9,1},... | collective-permute-start | bytes 49160 | tf_op jit(solution)/shard_map/ppermute | solution.py:285
  13.7 0.0 copy-start.4
  13.7 0.0 copy-start.5
  13.7 0.0 copy-start.6
  13.8 0.6 %copy-done.4 = f32[3,64]{1,0:T(4,128)S(1)} copy-done((f32[3,64]{1,0:T(4,128)S(1)}, f32[3,64]{1,0:T(4,128)}, u32[]{:S(2)}) %copy-start.4) | copy-done | bytes 792
  14.4 0.5 %prepare.1 = (bf16[1152,256]{1,0:T(8,128)(2,1)S(1)}, bf16[1152,256]{1,0:T(8,128)(2,1)S(1)}, bf16[64,64]{1,0:T(8,128)(2,1)S(1)}, bf16[3,64,256]{2,1,0:T(8,128)(2,...) custom-call(s32[1,8]{1,0:T(1,128)S(1)} %bitcast.11, bf16[9,33]{1,0:T(8,128)(2,1)S(1)} %copy-done.2, ...), custom_call_target="tpu_custom_call" | custom-call | flops 100000000 | bytes 10000000 | tf_op jit(solution)/shard_map/prepare/pallas_call | solution.py:289
  14.9 0.0 collective-permute-done.6.third
  14.9 0.0 collective-permute-done.5.second
  14.9 0.0 collective-permute-done.4.first
  14.9 0.3 %copy-done = bf16[3,64,192]{2,1,0:T(8,128)(2,1)S(1)} copy-done((bf16[3,64,192]{2,1,0:T(8,128)(2,1)S(1)}, bf16[3,64,192]{2,1,0:T(8,128)(2,1)}, u32[]{:S(2)}) %copy-start) | copy-done | bytes 73752
  15.3 2.8 %deblend.1 = (bf16[16,128]{1,0:T(8,128)(2,1)}, bf16[16,128]{1,0:T(8,128)(2,1)}) custom-call(bf16[2,16,256]{2,1,0:T(8,128)(2,1)S(1)} %pad_maximum_fusion.pair, bf16[2,16,256]{2,1,0:T(8,128)(2,1)S(1)} %collective-permute-done.4.first, bf16[2,16,256]{2,1,0:T(8,128)(2,1)S(1)} %collective-permute-done.5.second, ...), custom_call_target="tpu_custom_call" | custom-call | flops 400000000 | bytes 1000000 | tf_op jit(solution)/shard_map/deblend/pallas_call | solution.py:331
  (12 shorter events, 0.0 us)
Async XLA Ops:
  0.6 6.1 %collective-permute-start.1 = (bf16[1,16,128]{2,1,0:T(8,128)(2,1)}, bf16[1,16,128]{2,1,0:T(8,128)(2,1)S(1)}, u32[]{:S(2)}, u32[]{:S(2)}) collective-permute-start(bf16[1,16,128]{2,1,0:T(8,128)(2,1)} %param.11), channel_id=1, source_target_pairs={{0,4},{1,2},{2,1},{3,7},{4,0},{5,6},{6,5},{7,3},{8,12},{9,10},{10,... | collective-permute-start | bytes 12296 | tf_op jit(solution)/shard_map/ppermute | solution.py:285
  1.2 6.0 %collective-permute-start = (bf16[1,16,128]{2,1,0:T(8,128)(2,1)}, bf16[1,16,128]{2,1,0:T(8,128)(2,1)S(1)}, u32[]{:S(2)}, u32[]{:S(2)}) collective-permute-start(bf16[1,16,128]{2,1,0:T(8,128)(2,1)} %param.11), channel_id=1, source_target_pairs={{0,1},{1,0},{2,6},{3,7},{4,5},{5,4},{6,2},{7,3},{8,9},{9,8},{10,14... | collective-permute-start | bytes 12296 | tf_op jit(solution)/shard_map/ppermute | solution.py:285
  5.3 1.8 %collective-permute-start.2 = (bf16[1,16,128]{2,1,0:T(8,128)(2,1)}, bf16[1,16,128]{2,1,0:T(8,128)(2,1)S(1)}, u32[]{:S(2)}, u32[]{:S(2)}) collective-permute-start(bf16[1,16,128]{2,1,0:T(8,128)(2,1)} %param.11), channel_id=1, source_target_pairs={{0,4},{1,5},{2,3},{3,2},{4,0},{5,1},{6,7},{7,6},{8,12},{9,13},{10,... | collective-permute-start | bytes 12296 | tf_op jit(solution)/shard_map/ppermute | solution.py:285
  7.3 1.2 %collective-permute-start.3 = (bf16[1,16,256]{2,1,0:T(8,128)(2,1)S(1)}, bf16[1,16,256]{2,1,0:T(8,128)(2,1)S(1)}, u32[]{:S(2)}, u32[]{:S(2)}) collective-permute-start(bf16[1,16,256]{2,1,0:T(8,128)(2,1)S(1)} %frame.1), channel_id=1, source_target_pairs={{0,4},{1,5},{2,6},{3,7},{4,0},{5,1},{6,2},{7,3},{8,12},{9,13},{10,... | collective-permute-start | bytes 24584 | tf_op jit(solution)/shard_map/ppermute | solution.py:285
  8.5 5.3 %copy-start.2 = (bf16[9,33]{1,0:T(8,128)(2,1)S(1)}, bf16[9,33]{1,0:T(8,128)(2,1)}, u32[]{:S(2)}) copy-start(bf16[9,33]{1,0:T(8,128)(2,1)} %designature.1) | copy-start | bytes 1786
  8.5 5.3 %copy-start.3 = (bf16[9,33]{1,0:T(8,128)(2,1)S(1)}, bf16[9,33]{1,0:T(8,128)(2,1)}, u32[]{:S(2)}) copy-start(bf16[9,33]{1,0:T(8,128)(2,1)} %shaping.1) | copy-start | bytes 1786
  8.5 5.3 %copy-start.7 = (bf16[64]{0:T(256)(128)(2,1)S(1)}, bf16[64]{0:T(256)(128)(2,1)}, u32[]{:S(2)}) copy-start(bf16[64]{0:T(256)(128)(2,1)} %param.19) | copy-start | bytes 388
  8.5 5.3 %copy-start.1 = (bf16[64,30]{0,1:T(8,128)(2,1)S(1)}, bf16[64,30]{0,1:T(8,128)(2,1)}, u32[]{:S(2)}) copy-start(bf16[64,30]{0,1:T(8,128)(2,1)} %param.15) | copy-start | bytes 11524
  8.5 6.4 %collective-permute-start.6 = (bf16[2,16,256]{2,1,0:T(8,128)(2,1)S(1)}, bf16[2,16,256]{2,1,0:T(8,128)(2,1)S(1)}, u32[]{:S(2)}, u32[]{:S(2)}) collective-permute-start(bf16[2,16,256]{2,1,0:T(8,128)(2,1)S(1)} %pad_maximum_fusion.pair), channel_id=1, source_target_pairs={{0,4},{1,5},{2,6},{3,7},{4,0},{5,1},{6,2},{7,3},{8,12},{9,13},{10,... | collective-permute-start | bytes 49160 | tf_op jit(solution)/shard_map/ppermute | solution.py:285
  8.7 6.1 %collective-permute-start.5 = (bf16[2,16,256]{2,1,0:T(8,128)(2,1)S(1)}, bf16[2,16,256]{2,1,0:T(8,128)(2,1)S(1)}, u32[]{:S(2)}, u32[]{:S(2)}) collective-permute-start(bf16[2,16,256]{2,1,0:T(8,128)(2,1)S(1)} %pad_maximum_fusion.pair), channel_id=1, source_target_pairs={{0,4},{1,5},{2,6},{3,7},{4,0},{5,1},{6,2},{7,3},{8,16},{9,17},{10,... | collective-permute-start | bytes 49160 | tf_op jit(solution)/shard_map/ppermute | solution.py:285
  9.1 5.9 %collective-permute-start.4 = (bf16[2,16,256]{2,1,0:T(8,128)(2,1)S(1)}, bf16[2,16,256]{2,1,0:T(8,128)(2,1)S(1)}, u32[]{:S(2)}, u32[]{:S(2)}) collective-permute-start(bf16[2,16,256]{2,1,0:T(8,128)(2,1)S(1)} %pad_maximum_fusion.pair), channel_id=1, source_target_pairs={{0,8},{1,9},{2,10},{3,11},{4,12},{5,13},{6,14},{7,15},{8,0},{9,1},... | collective-permute-start | bytes 49160 | tf_op jit(solution)/shard_map/ppermute | solution.py:285
  13.7 0.7 %copy-start.4 = (f32[3,64]{1,0:T(4,128)S(1)}, f32[3,64]{1,0:T(4,128)}, u32[]{:S(2)}) copy-start(f32[3,64]{1,0:T(4,128)} %hidden_bias.1) | copy-start | bytes 2308
  13.7 0.7 %copy-start.5 = (s32[8]{0:T(128)S(1)}, s32[8]{0:T(128)}, u32[]{:S(2)}) copy-start(s32[8]{0:T(128)} %param.13) | copy-start | bytes 100
  13.7 0.7 %copy-start.6 = (f32[64]{0:T(128)S(1)}, f32[64]{0:T(128)}, u32[]{:S(2)}) copy-start(f32[64]{0:T(128)} %param.16) | copy-start | bytes 772
  14.4 0.9 %copy-start = (bf16[3,64,192]{2,1,0:T(8,128)(2,1)S(1)}, bf16[3,64,192]{2,1,0:T(8,128)(2,1)}, u32[]{:S(2)}) copy-start(bf16[3,64,192]{2,1,0:T(8,128)(2,1)} %hidden.1) | copy-start | bytes 221188

commit v6 on v5

--- a/solution.py
+++ b/solution.py
@@ -121,13 +121,11 @@
     left = jnp.where(t == 0, 0.0, pick((t + 2) % 3, got))
     right = jnp.where(t == parts - 1, 0.0, pick(t % 3, got))
     left, right = jnp.where(alive, left, DEAD), jnp.where(alive, right, DEAD)
-    gap = jnp.zeros((x.shape[0], span - samples), F32)
-    lanes = lax.broadcasted_iota(jnp.int32, (x.shape[0], span), 1)
-    spread = [jnp.concatenate([v, gap], axis=1) for v in (left, x, right)]
-    left = pltpu.roll(spread[0], span + BEFORE - samples, 1)
-    x, right = pltpu.roll(spread[1], BEFORE, 1), pltpu.roll(spread[2], (BEFORE + samples) % span, 1)
-    x = jnp.where(lanes < BEFORE, left, jnp.where(lanes < BEFORE + samples, x, right))
-    out[0] = x.astype(BF16)
+    tiles = [left[:, samples - LANES :]] + [x[:, v : v + LANES] for v in range(0, samples, LANES)] + [right[:, 0:LANES]]
+    turned = [pltpu.roll(v, BEFORE, 1) for v in tiles]
+    ahead = lax.broadcasted_iota(jnp.int32, tiles[0].shape, 1) < BEFORE
+    for w in range(span // LANES):
+        out[0, :, w * LANES : (w + 1) * LANES] = jnp.where(ahead, turned[w], turned[w + 1]).astype(BF16)
 
 
 def moved(tiles, by):
@@ -175,8 +173,6 @@
     lowest, highest = chip == 0, chip == shots // 2 - 1
     zero = jnp.zeros((nodes, LANES), F32)
     depth = hidden.shape[2]
-    wh[...] = wx[...]
-    wh[:, :, 0:depth] = hidden[...]
     odd = s % 2 == 1
     alive = pair[0].astype(F32)[:, BEFORE : BEFORE + 1] < LIMIT
     near = [[jnp.where(odd, v[1 - j].astype(F32), v[j].astype(F32)) for j in range(2)] for v in (pair, first, second, third)]
@@ -215,6 +211,8 @@
         for n in range(nodes):
             f = jnp.where(live[n * 8 : n * 8 + 8, :] & inside, sums[w][n], 0.0)
             gs[(w * nodes + n) * 16 : (w * nodes + n) * 16 + 8, :] = f.astype(BF16).astype(F32)
+    wh[...] = wx[...]
+    wh[:, :, 0:depth] = hidden[...]
     delays = small[1:2, :]
     lane = lax.broadcasted_iota(jnp.int32, (1, LANES), 1)
     own = []

time: 18.3 us -> 18.3 us (level)
  no operation moved by 1% of the time
where the time goes in v6:
time: 18.3 us; the launch traced here: 18.1 us
  starting transfers between devices  9.36 us (51%)
  Pallas kernels  3.47 us (19%)
  waiting for transfers between devices  1.5 us (8%)
  other arithmetic  1.42 us (8%)
  between operations  1.38 us (8%)
  local copies, waits for them, and re-layouts  0.99 us (5%)
    ppermute x7, starting transfers between devices, send(): return lax.ppermute(x, AXES, pairs)  9.36 us
    pallas_call x1, Pallas kernels, local(): pl.pallas_call(functools.partial(deblend, total, shots), out_shape=(jax.S...  2.85 us
    ppermute x7, waiting for transfers between devices, send(): return lax.ppermute(x, AXES, pairs)  1.5 us
    unnamed x16, local copies, waits for them, and re-layouts  0.99 us
    select_n x1, other arithmetic, local(): mine = lax.optimization_barrier(jnp.where(keep, records, dead))  0.76 us
    gt x1, other arithmetic, local(): keep = live[:, :, None] > 0  0.66 us
    pallas_call x1, Pallas kernels, local(): pl.pallas_call(prepare, out_shape=(jax.ShapeDtypeStruct((FN * LANES, wind...  0.48 us
  transfers between devices with their start and end apart: 7, of which 2 were waited for; matrix products, arithmetic and copies ran while one was open for 8% of the time, Pallas kernels for 3%

profile of v6, /device:TPU:0, one launch (start us, length us, event | category | flops | bytes accessed | tf_op | source)
XLA Modules:
  0.0 18.1 jit_solution(17346789793762251205)
XLA Ops:
  0.6 0.6 %collective-permute-start.1 = (bf16[1,16,128]{2,1,0:T(8,128)(2,1)}, bf16[1,16,128]{2,1,0:T(8,128)(2,1)S(1)}, u32[]{:S(2)}, u32[]{:S(2)}) collective-permute-start(bf16[1,16,128]{2,1,0:T(8,128)(2,1)} %param.11), channel_id=1, source_target_pairs={{0,4},{1,2},{2,1},{3,7},{4,0},{5,6},{6,5},{7,3},{8,12},{9,10},{10,... | collective-permute-start | bytes 12296 | tf_op jit(solution)/shard_map/ppermute | solution.py:283
  1.2 4.1 %collective-permute-start = (bf16[1,16,128]{2,1,0:T(8,128)(2,1)}, bf16[1,16,128]{2,1,0:T(8,128)(2,1)S(1)}, u32[]{:S(2)}, u32[]{:S(2)}) collective-permute-start(bf16[1,16,128]{2,1,0:T(8,128)(2,1)} %param.11), channel_id=1, source_target_pairs={{0,1},{1,0},{2,6},{3,7},{4,5},{5,4},{6,2},{7,3},{8,9},{9,8},{10,14... | collective-permute-start | bytes 12296 | tf_op jit(solution)/shard_map/ppermute | solution.py:283
  5.3 0.0 collective-permute-start.2
  5.3 0.7 %compare_bitcast_fusion = pred[16]{0:T(512)(128)(4,1)S(1)} fusion(s32[1,16]{1,0:T(1,128)} %param.12), kind=kLoop, calls=%fused_computation.2 | loop fusion | flops 16 | bytes 80 | tf_op jit(solution)/shard_map/gt | solution.py:314
  6.0 0.8 %broadcast_select_fusion.mine = bf16[1,16,128]{2,1,0:T(8,128)(2,1)S(1)} fusion(bf16[1,16,128]{2,1,0:T(8,128)(2,1)} %param.11, pred[16]{0:T(512)(128)(4,1)S(1)} %compare_bitcast_fusion), kind=kLoop, calls=%fused_computation.1 | loop fusion | flops 2048 | bytes 8208 | tf_op jit(solution)/shard_map/jit(_where)/select_n | solution.py:317
  6.7 0.0 collective-permute-done.1.second
  6.8 0.4 %collective-permute-done.first = bf16[1,16,128]{2,1,0:T(8,128)(2,1)S(1)} collective-permute-done((bf16[1,16,128]{2,1,0:T(8,128)(2,1)}, bf16[1,16,128]{2,1,0:T(8,128)(2,1)S(1)}, u32[]{:S(2)}, u32[]{:S(2)}) %collective-permute-start) | collective-permute-done | bytes 4128 | tf_op jit(solution)/shard_map/ppermute | solution.py:283
  7.2 0.1 frame.1
  7.3 0.1 collective-permute-start.3
  7.4 1.1 %collective-permute-done.3 = bf16[1,16,256]{2,1,0:T(8,128)(2,1)S(1)} collective-permute-done((bf16[1,16,256]{2,1,0:T(8,128)(2,1)S(1)}, bf16[1,16,256]{2,1,0:T(8,128)(2,1)S(1)}, u32[]{:S(2)}, u32[]{:S(2)}) %collective-permute-start.3) | collective-permute-done | bytes 8224 | tf_op jit(solution)/shard_map/ppermute | solution.py:283
  8.5 0.0 copy-start.1
  8.5 0.2 %collective-permute-start.6 = (bf16[2,16,256]{2,1,0:T(8,128)(2,1)S(1)}, bf16[2,16,256]{2,1,0:T(8,128)(2,1)S(1)}, u32[]{:S(2)}, u32[]{:S(2)}) collective-permute-start(bf16[2,16,256]{2,1,0:T(8,128)(2,1)S(1)} %pad_maximum_fusion.pair), channel_id=1, source_target_pairs={{0,4},{1,5},{2,6},{3,7},{4,0},{5,1},{6,2},{7,3},{8,12},{9,13},{10,... | collective-permute-start | bytes 49160 | tf_op jit(solution)/shard_map/ppermute | solution.py:283
  8.7 0.3 %collective-permute-start.5 = (bf16[2,16,256]{2,1,0:T(8,128)(2,1)S(1)}, bf16[2,16,256]{2,1,0:T(8,128)(2,1)S(1)}, u32[]{:S(2)}, u32[]{:S(2)}) collective-permute-start(bf16[2,16,256]{2,1,0:T(8,128)(2,1)S(1)} %pad_maximum_fusion.pair), channel_id=1, source_target_pairs={{0,4},{1,5},{2,6},{3,7},{4,0},{5,1},{6,2},{7,3},{8,16},{9,17},{10,... | collective-permute-start | bytes 49160 | tf_op jit(solution)/shard_map/ppermute | solution.py:283
  9.1 4.0 %collective-permute-start.4 = (bf16[2,16,256]{2,1,0:T(8,128)(2,1)S(1)}, bf16[2,16,256]{2,1,0:T(8,128)(2,1)S(1)}, u32[]{:S(2)}, u32[]{:S(2)}) collective-permute-start(bf16[2,16,256]{2,1,0:T(8,128)(2,1)S(1)} %pad_maximum_fusion.pair), channel_id=1, source_target_pairs={{0,8},{1,9},{2,10},{3,11},{4,12},{5,13},{6,14},{7,15},{8,0},{9,1},... | collective-permute-start | bytes 49160 | tf_op jit(solution)/shard_map/ppermute | solution.py:283
  13.7 0.0 copy-start.4
  13.7 0.0 copy-start.5
  13.7 0.0 copy-start.6
  13.8 0.6 %copy-done.4 = f32[3,64]{1,0:T(4,128)S(1)} copy-done((f32[3,64]{1,0:T(4,128)S(1)}, f32[3,64]{1,0:T(4,128)}, u32[]{:S(2)}) %copy-start.4) | copy-done | bytes 792
  14.4 0.5 %prepare.1 = (bf16[1152,256]{1,0:T(8,128)(2,1)S(1)}, bf16[1152,256]{1,0:T(8,128)(2,1)S(1)}, bf16[64,64]{1,0:T(8,128)(2,1)S(1)}, bf16[3,64,256]{2,1,0:T(8,128)(2,...) custom-call(s32[1,8]{1,0:T(1,128)S(1)} %bitcast.11, bf16[9,33]{1,0:T(8,128)(2,1)S(1)} %copy-done.2, ...), custom_call_target="tpu_custom_call" | custom-call | flops 100000000 | bytes 10000000 | tf_op jit(solution)/shard_map/prepare/pallas_call | solution.py:287
  14.9 0.0 collective-permute-done.6.third
  14.9 0.0 collective-permute-done.5.second
  14.9 0.0 collective-permute-done.4.first
  14.9 0.3 %copy-done = bf16[3,64,192]{2,1,0:T(8,128)(2,1)S(1)} copy-done((bf16[3,64,192]{2,1,0:T(8,128)(2,1)S(1)}, bf16[3,64,192]{2,1,0:T(8,128)(2,1)}, u32[]{:S(2)}) %copy-start) | copy-done | bytes 73752
  15.3 2.8 %deblend.1 = (bf16[16,128]{1,0:T(8,128)(2,1)}, bf16[16,128]{1,0:T(8,128)(2,1)}) custom-call(bf16[2,16,256]{2,1,0:T(8,128)(2,1)S(1)} %pad_maximum_fusion.pair, bf16[2,16,256]{2,1,0:T(8,128)(2,1)S(1)} %collective-permute-done.4.first, bf16[2,16,256]{2,1,0:T(8,128)(2,1)S(1)} %collective-permute-done.5.second, ...), custom_call_target="tpu_custom_call" | custom-call | flops 400000000 | bytes 1000000 | tf_op jit(solution)/shard_map/deblend/pallas_call | solution.py:329
  (12 shorter events, 0.0 us)
Async XLA Ops:
  0.6 6.1 %collective-permute-start.1 = (bf16[1,16,128]{2,1,0:T(8,128)(2,1)}, bf16[1,16,128]{2,1,0:T(8,128)(2,1)S(1)}, u32[]{:S(2)}, u32[]{:S(2)}) collective-permute-start(bf16[1,16,128]{2,1,0:T(8,128)(2,1)} %param.11), channel_id=1, source_target_pairs={{0,4},{1,2},{2,1},{3,7},{4,0},{5,6},{6,5},{7,3},{8,12},{9,10},{10,... | collective-permute-start | bytes 12296 | tf_op jit(solution)/shard_map/ppermute | solution.py:283
  1.2 6.0 %collective-permute-start = (bf16[1,16,128]{2,1,0:T(8,128)(2,1)}, bf16[1,16,128]{2,1,0:T(8,128)(2,1)S(1)}, u32[]{:S(2)}, u32[]{:S(2)}) collective-permute-start(bf16[1,16,128]{2,1,0:T(8,128)(2,1)} %param.11), channel_id=1, source_target_pairs={{0,1},{1,0},{2,6},{3,7},{4,5},{5,4},{6,2},{7,3},{8,9},{9,8},{10,14... | collective-permute-start | bytes 12296 | tf_op jit(solution)/shard_map/ppermute | solution.py:283
  5.3 1.8 %collective-permute-start.2 = (bf16[1,16,128]{2,1,0:T(8,128)(2,1)}, bf16[1,16,128]{2,1,0:T(8,128)(2,1)S(1)}, u32[]{:S(2)}, u32[]{:S(2)}) collective-permute-start(bf16[1,16,128]{2,1,0:T(8,128)(2,1)} %param.11), channel_id=1, source_target_pairs={{0,4},{1,5},{2,3},{3,2},{4,0},{5,1},{6,7},{7,6},{8,12},{9,13},{10,... | collective-permute-start | bytes 12296 | tf_op jit(solution)/shard_map/ppermute | solution.py:283
  7.3 1.2 %collective-permute-start.3 = (bf16[1,16,256]{2,1,0:T(8,128)(2,1)S(1)}, bf16[1,16,256]{2,1,0:T(8,128)(2,1)S(1)}, u32[]{:S(2)}, u32[]{:S(2)}) collective-permute-start(bf16[1,16,256]{2,1,0:T(8,128)(2,1)S(1)} %frame.1), channel_id=1, source_target_pairs={{0,4},{1,5},{2,6},{3,7},{4,0},{5,1},{6,2},{7,3},{8,12},{9,13},{10,... | collective-permute-start | bytes 24584 | tf_op jit(solution)/shard_map/ppermute | solution.py:283
  8.5 5.3 %copy-start.2 = (bf16[9,33]{1,0:T(8,128)(2,1)S(1)}, bf16[9,33]{1,0:T(8,128)(2,1)}, u32[]{:S(2)}) copy-start(bf16[9,33]{1,0:T(8,128)(2,1)} %designature.1) | copy-start | bytes 1786
  8.5 5.3 %copy-start.3 = (bf16[9,33]{1,0:T(8,128)(2,1)S(1)}, bf16[9,33]{1,0:T(8,128)(2,1)}, u32[]{:S(2)}) copy-start(bf16[9,33]{1,0:T(8,128)(2,1)} %shaping.1) | copy-start | bytes 1786
  8.5 5.3 %copy-start.7 = (bf16[64]{0:T(256)(128)(2,1)S(1)}, bf16[64]{0:T(256)(128)(2,1)}, u32[]{:S(2)}) copy-start(bf16[64]{0:T(256)(128)(2,1)} %param.19) | copy-start | bytes 388
  8.5 5.3 %copy-start.1 = (bf16[64,30]{0,1:T(8,128)(2,1)S(1)}, bf16[64,30]{0,1:T(8,128)(2,1)}, u32[]{:S(2)}) copy-start(bf16[64,30]{0,1:T(8,128)(2,1)} %param.15) | copy-start | bytes 11524
  8.5 6.4 %collective-permute-start.6 = (bf16[2,16,256]{2,1,0:T(8,128)(2,1)S(1)}, bf16[2,16,256]{2,1,0:T(8,128)(2,1)S(1)}, u32[]{:S(2)}, u32[]{:S(2)}) collective-permute-start(bf16[2,16,256]{2,1,0:T(8,128)(2,1)S(1)} %pad_maximum_fusion.pair), channel_id=1, source_target_pairs={{0,4},{1,5},{2,6},{3,7},{4,0},{5,1},{6,2},{7,3},{8,12},{9,13},{10,... | collective-permute-start | bytes 49160 | tf_op jit(solution)/shard_map/ppermute | solution.py:283
  8.7 6.1 %collective-permute-start.5 = (bf16[2,16,256]{2,1,0:T(8,128)(2,1)S(1)}, bf16[2,16,256]{2,1,0:T(8,128)(2,1)S(1)}, u32[]{:S(2)}, u32[]{:S(2)}) collective-permute-start(bf16[2,16,256]{2,1,0:T(8,128)(2,1)S(1)} %pad_maximum_fusion.pair), channel_id=1, source_target_pairs={{0,4},{1,5},{2,6},{3,7},{4,0},{5,1},{6,2},{7,3},{8,16},{9,17},{10,... | collective-permute-start | bytes 49160 | tf_op jit(solution)/shard_map/ppermute | solution.py:283
  9.1 5.9 %collective-permute-start.4 = (bf16[2,16,256]{2,1,0:T(8,128)(2,1)S(1)}, bf16[2,16,256]{2,1,0:T(8,128)(2,1)S(1)}, u32[]{:S(2)}, u32[]{:S(2)}) collective-permute-start(bf16[2,16,256]{2,1,0:T(8,128)(2,1)S(1)} %pad_maximum_fusion.pair), channel_id=1, source_target_pairs={{0,8},{1,9},{2,10},{3,11},{4,12},{5,13},{6,14},{7,15},{8,0},{9,1},... | collective-permute-start | bytes 49160 | tf_op jit(solution)/shard_map/ppermute | solution.py:283
  13.7 0.7 %copy-start.4 = (f32[3,64]{1,0:T(4,128)S(1)}, f32[3,64]{1,0:T(4,128)}, u32[]{:S(2)}) copy-start(f32[3,64]{1,0:T(4,128)} %hidden_bias.1) | copy-start | bytes 2308
  13.7 0.7 %copy-start.5 = (s32[8]{0:T(128)S(1)}, s32[8]{0:T(128)}, u32[]{:S(2)}) copy-start(s32[8]{0:T(128)} %param.13) | copy-start | bytes 100
  13.7 0.7 %copy-start.6 = (f32[64]{0:T(128)S(1)}, f32[64]{0:T(128)}, u32[]{:S(2)}) copy-start(f32[64]{0:T(128)} %param.16) | copy-start | bytes 772
  14.4 0.9 %copy-start = (bf16[3,64,192]{2,1,0:T(8,128)(2,1)S(1)}, bf16[3,64,192]{2,1,0:T(8,128)(2,1)}, u32[]{:S(2)}) copy-start(bf16[3,64,192]{2,1,0:T(8,128)(2,1)} %hidden.1) | copy-start | bytes 221188
